TPU v7x, 32 devices: a whole 2x2x4 slice. The times are simulated.
32 devices in a mesh: fsdp: 8 (over y, x, core), tp: 4 (over z).
Axes of the slice: x: 2, y: 2, z: 4, core: 2. Of those that a mesh axis runs over, the one named last changes fastest.
Arguments:
- tokens: bfloat16 [2, 8, 1024, 2048], P(None, 'fsdp', 'tp'), may hold values from -6 to 6
- segment: int32 [2, 8, 1024], P(None, 'fsdp'), may hold values from 0 to 7, never falling along the last dimension, each value on 1 to 512 neighbouring positions
- ln1_gain: float32 [2048], P(('fsdp', 'tp')), may hold values from 0.5 to 1.5
- ln1_bias: float32 [2048], P(('fsdp', 'tp')), may hold values from -1.5 to 1.5
- w_query: bfloat16 [2048, 2048], P('fsdp', 'tp'), may hold values from -0.125 to 0.125
- w_key: bfloat16 [2048, 2048], P('fsdp', 'tp'), may hold values from -0.125 to 0.125
- w_value: bfloat16 [2048, 4096], P('fsdp', 'tp'), may hold values from -0.125 to 0.125
- w_gate: bfloat16 [2048, 4096], P('fsdp', 'tp'), may hold values from -0.125 to 0.125
- w_output: bfloat16 [4096, 2048], P('tp', 'fsdp'), may hold values from -0.09375 to 0.09375
- gn_gain: float32 [4096], P(('fsdp', 'tp')), may hold values from 0.5 to 1.5
- gn_bias: float32 [4096], P(('fsdp', 'tp')), may hold values from -1.5 to 1.5
- ln2_gain: float32 [2048], P(('fsdp', 'tp')), may hold values from 0.5 to 1.5
- ln2_bias: float32 [2048], P(('fsdp', 'tp')), may hold values from -1.5 to 1.5
- w_inner: bfloat16 [2048, 4096], P('fsdp', 'tp'), may hold values from -0.125 to 0.125
- b_inner: float32 [4096], P(('fsdp', 'tp')), may hold values from -1.5 to 1.5
- w_outer: bfloat16 [4096, 2048], P('tp', 'fsdp'), may hold values from -0.09375 to 0.09375
- b_outer: float32 [2048], P(('fsdp', 'tp')), may hold values from -1.5 to 1.5
- cotangent: bfloat16 [2, 8, 1024, 2048], P(None, 'fsdp', 'tp'), may hold values from -6 to 6
Outputs:
- out: bfloat16 [2, 8, 1024, 2048], P(None, 'fsdp', 'tp')
- input_grad: float32 [2, 8, 1024, 2048], P(None, 'fsdp', 'tp')
- grad_ln1_gain: float32 [2048], P(('fsdp', 'tp'))
- grad_ln1_bias: float32 [2048], P(('fsdp', 'tp'))
- grad_w_query: float32 [2048, 2048], P('fsdp', 'tp')
- grad_w_key: float32 [2048, 2048], P('fsdp', 'tp')
- grad_w_value: float32 [2048, 4096], P('fsdp', 'tp')
- grad_w_gate: float32 [2048, 4096], P('fsdp', 'tp')
- grad_w_output: float32 [4096, 2048], P('tp', 'fsdp')
- grad_gn_gain: float32 [4096], P(('fsdp', 'tp'))
- grad_gn_bias: float32 [4096], P(('fsdp', 'tp'))
- grad_ln2_gain: float32 [2048], P(('fsdp', 'tp'))
- grad_ln2_bias: float32 [2048], P(('fsdp', 'tp'))
- grad_w_inner: float32 [2048, 4096], P('fsdp', 'tp')
- grad_b_inner: float32 [4096], P(('fsdp', 'tp'))
- grad_w_outer: float32 [4096, 2048], P('tp', 'fsdp')
- grad_b_outer: float32 [2048], P(('fsdp', 'tp'))
Inputs may be any that keep to these rules, and one draw needn't show every extreme that they name: `segment`: along a sequence the document numbers never fall; a document spans 1 to 512 tokens.
All inputs are finite; a program needn't handle non-finite values.
Results may differ from a plain program's by a relative error of at most 0.018.
Values may be sent and summed in bfloat16 or wider, within the bound.
A program may use at most 320 MiB of HBM per device.

v0:
```python
import jax
import jax.numpy as jnp
from jax import lax
from jax.sharding import PartitionSpec as P

DK = 256
DV = 512
STRETCH = 512
MB = 2


EPSILON = 1e-05
GROUP_EPSILON = 0.25


def layer_norm(values, scaling, offset):
    centred = values - jnp.mean(values, axis=-1, keepdims=True)
    variance = jnp.mean(centred * centred, axis=-1, keepdims=True)
    return centred * lax.rsqrt(variance + EPSILON) * scaling + offset


def gate_norm(retained, gate_pre, scaling, offset):
    length = retained.shape[0]
    centred = retained - jnp.mean(retained, axis=-1, keepdims=True)
    variance = jnp.mean(centred * centred, axis=-1, keepdims=True)
    grouped = (centred * lax.rsqrt(variance + GROUP_EPSILON)).reshape(length, -1) * scaling + offset
    return gate_pre * jax.nn.sigmoid(gate_pre) * grouped


def exact_gelu(values):
    return jax.nn.gelu(values, approximate=False)


def rotate(values, position, turning):
    half_dim = values.shape[-1] // 2
    frequency = 10000.0 ** (-jnp.arange(half_dim, dtype=jnp.float32) / half_dim)
    angles = position[:, None] * frequency[None, :] * turning
    cosine = jnp.cos(angles)[:, None, :]
    sinusoid = jnp.sin(angles)[:, None, :]
    leading = values[..., :half_dim]
    trailing = values[..., half_dim:]
    return jnp.concatenate(
        [leading * cosine - trailing * sinusoid, leading * sinusoid + trailing * cosine], axis=-1
    )


def doc_positions(segments):
    length = segments.shape[0]
    indices = jnp.arange(length, dtype=jnp.int32)
    previous = jnp.concatenate([jnp.full((1,), -1, jnp.int32), segments[:-1]])
    starts = lax.cummax(jnp.where(segments != previous, indices, 0), axis=0)
    return (indices - starts).astype(jnp.float32)


def decay_mask(first_row, segments, log_decay):
    row_ids = first_row + jnp.arange(STRETCH, dtype=jnp.int32)
    columns = jnp.arange(segments.shape[0], dtype=jnp.int32)
    seg_query = lax.dynamic_slice_in_dim(segments, first_row, STRETCH, 0)
    distance = row_ids[:, None] - columns[None, :]
    allowed = (distance >= 0) & (seg_query[:, None] == segments[None, :])
    steps_back = jnp.maximum(distance, 0).astype(jnp.float32)
    return jnp.where(allowed[None], jnp.exp(steps_back[None] * log_decay[:, None, None]), 0.0)


def row_product(left, right):
    return lax.dot_general(
        left, right, (((0,), (0,)), ((), ())), preferred_element_type=jnp.float32
    )


def back_product(left, right):
    return lax.dot_general(
        left, right, (((1,), (1,)), ((), ())), preferred_element_type=jnp.float32
    )


def fetch_mixer(w_query, w_key, w_value, w_gate, w_output):
    return (
        lax.all_gather(w_query, "fsdp", axis=0, tiled=True),
        lax.all_gather(w_key, "fsdp", axis=0, tiled=True),
        lax.all_gather(w_value, "fsdp", axis=0, tiled=True),
        lax.all_gather(w_gate, "fsdp", axis=0, tiled=True),
        lax.all_gather(w_output, "fsdp", axis=1, tiled=True),
    )


def fetch_ffn(w_inner, w_outer):
    return (
        lax.all_gather(w_inner, "fsdp", axis=0, tiled=True),
        lax.all_gather(w_outer, "fsdp", axis=1, tiled=True),
    )


def shards(
    tokens,
    segment,
    ln1_gain,
    ln1_bias,
    w_query,
    w_key,
    w_value,
    w_gate,
    w_output,
    gn_gain,
    gn_bias,
    ln2_gain,
    ln2_bias,
    w_inner,
    b_inner,
    w_outer,
    b_outer,
    cotangent,
):
    tp_index = lax.axis_index("tp")
    model_width = tokens.shape[3]
    query_cols = w_query.shape[1]
    value_cols = w_value.shape[1]
    inner_cols = w_inner.shape[1]
    heads_here = query_cols // DK
    score_scale = DK ** (-0.5)
    vectors = (
        lax.all_gather(ln1_gain, ("fsdp", "tp"), axis=0, tiled=True),
        lax.all_gather(ln1_bias, ("fsdp", "tp"), axis=0, tiled=True),
        lax.all_gather(ln2_gain, ("fsdp", "tp"), axis=0, tiled=True),
        lax.all_gather(ln2_bias, ("fsdp", "tp"), axis=0, tiled=True),
        lax.all_gather(b_outer, ("fsdp", "tp"), axis=0, tiled=True),
        lax.all_gather(b_inner, ("fsdp", "tp"), axis=0, tiled=True),
        lax.all_gather(gn_gain, ("fsdp", "tp"), axis=0, tiled=True),
        lax.all_gather(gn_bias, ("fsdp", "tp"), axis=0, tiled=True),
    )
    (
        norm1_gain,
        norm1_bias,
        norm2_gain,
        second_norm_bias,
        outer_bias,
        inner_all,
        group_gain_all,
        group_bias_all,
    ) = vectors
    inner_bias = lax.dynamic_slice_in_dim(inner_all, tp_index * inner_cols, inner_cols, 0)
    group_gain = lax.dynamic_slice_in_dim(group_gain_all, tp_index * value_cols, value_cols, 0)
    group_bias = lax.dynamic_slice_in_dim(group_bias_all, tp_index * value_cols, value_cols, 0)
    head_ids = (tp_index * heads_here + jnp.arange(heads_here, dtype=jnp.int32)).astype(jnp.float32)
    log_decay = jnp.log1p(-(2.0 ** (-5.0 - head_ids)))
    inner_total = jnp.zeros((model_width, inner_cols), jnp.float32)
    outer_total = jnp.zeros((inner_cols, model_width), jnp.float32)
    bias_total = jnp.zeros((inner_cols,), jnp.float32)
    totals = {
        "query": jnp.zeros((model_width, query_cols), jnp.float32),
        "key": jnp.zeros((model_width, query_cols), jnp.float32),
        "value": jnp.zeros((model_width, value_cols), jnp.float32),
        "gate": jnp.zeros((model_width, value_cols), jnp.float32),
        "output": jnp.zeros((value_cols, model_width), jnp.float32),
        "inner": inner_total,
        "outer": outer_total,
        "norm1_gain": jnp.zeros((model_width,), jnp.float32),
        "norm1_bias": jnp.zeros((model_width,), jnp.float32),
        "norm2_gain": jnp.zeros((model_width,), jnp.float32),
        "norm2_bias": jnp.zeros((model_width,), jnp.float32),
        "outer_bias": jnp.zeros((model_width,), jnp.float32),
        "inner_bias": bias_total,
        "group_gain": jnp.zeros((value_cols,), jnp.float32),
        "group_bias": jnp.zeros((value_cols,), jnp.float32),
    }
    out_rows = []
    input_rows = []
    for micro_batch in range(MB):
        rows_in = tokens[micro_batch, 0].astype(jnp.float32)
        segments = segment[micro_batch, 0]
        position = doc_positions(segments)
        mixer_now = fetch_mixer(w_query, w_key, w_value, w_gate, w_output)
        query_full, key_full, value_full, gate_full, output_full = mixer_now
        normed_one, norm1_back = jax.vjp(layer_norm, rows_in, norm1_gain, norm1_bias)
        normed_all = lax.all_gather(normed_one.astype(jnp.bfloat16), "tp", axis=0, tiled=True)
        length = normed_all.shape[0]
        block_ids = jnp.arange(length // STRETCH, dtype=jnp.int32)
        query_pre = jnp.dot(normed_all, query_full, preferred_element_type=jnp.float32)
        key_pre = jnp.dot(normed_all, key_full, preferred_element_type=jnp.float32)
        gate_pre = jnp.dot(normed_all, gate_full, preferred_element_type=jnp.float32)
        value_rounded = jnp.dot(normed_all, value_full, preferred_element_type=jnp.float32).astype(
            jnp.bfloat16
        )
        value_rounded = value_rounded.reshape(length, heads_here, DV)
        query_low = rotate(query_pre.reshape(length, heads_here, DK), position, 1.0).astype(
            jnp.bfloat16
        )
        key_rounded = rotate(key_pre.reshape(length, heads_here, DK), position, 1.0).astype(
            jnp.bfloat16
        )

        def forward_block(block_id):
            first_row = block_id * STRETCH
            query_tile_rows = lax.dynamic_slice_in_dim(query_low, first_row, STRETCH, 0)
            masking = decay_mask(first_row, segments, log_decay)
            retention_scores = jnp.einsum(
                "awx,bwx->wab", query_tile_rows, key_rounded, preferred_element_type=jnp.float32
            )
            weights_low = (retention_scores * masking * score_scale).astype(jnp.bfloat16)
            return jnp.einsum(
                "hnm,mhe->nhe", weights_low, value_rounded, preferred_element_type=jnp.float32
            )

        retained = lax.map(forward_block, block_ids).reshape(length, heads_here, DV)
        gated, gate_back = jax.vjp(gate_norm, retained, gate_pre, group_gain, group_bias)
        gated_low = gated.astype(jnp.bfloat16)
        hidden = rows_in + lax.psum_scatter(
            jnp.dot(gated_low, output_full, preferred_element_type=jnp.float32),
            "tp",
            scatter_dimension=0,
            tiled=True,
        )
        normed_two, norm2_back = jax.vjp(layer_norm, hidden, norm2_gain, second_norm_bias)
        grad_rows = cotangent[micro_batch, 0]
        totals["outer_bias"] = totals["outer_bias"] + jnp.sum(grad_rows.astype(jnp.float32), axis=0)
        ffn_now = fetch_ffn(w_inner, w_outer)
        inner_full, outer_full = ffn_now
        normed_two_all = lax.all_gather(normed_two.astype(jnp.bfloat16), "tp", axis=0, tiled=True)
        inner_pre = (
            jnp.dot(normed_two_all, inner_full, preferred_element_type=jnp.float32) + inner_bias
        )
        active, gelu_back = jax.vjp(exact_gelu, inner_pre)
        active_low = active.astype(jnp.bfloat16)
        result = (
            hidden
            + lax.psum_scatter(
                jnp.dot(active_low, outer_full, preferred_element_type=jnp.float32).astype(
                    jnp.bfloat16
                ),
                "tp",
                scatter_dimension=0,
                tiled=True,
            ).astype(jnp.float32)
            + outer_bias
        )
        out_rows.append(result.astype(jnp.bfloat16))
        ffn_back = fetch_ffn(w_inner, w_outer)
        inner_back, outer_back = ffn_back
        grad_all = lax.all_gather(grad_rows, "tp", axis=0, tiled=True)
        totals["outer"] = totals["outer"] + row_product(active_low, grad_all)
        inner_grad = gelu_back(back_product(grad_all, outer_back))[0]
        inner_grad_low = inner_grad.astype(jnp.bfloat16)
        totals["inner_bias"] = totals["inner_bias"] + jnp.sum(
            inner_grad_low.astype(jnp.float32), axis=0
        )
        totals["inner"] = totals["inner"] + row_product(normed_two_all, inner_grad_low)
        normed_two_grad = lax.psum_scatter(
            back_product(inner_grad_low, inner_back), "tp", scatter_dimension=0, tiled=True
        )
        hidden_part, gain2_part, bias2_part = norm2_back(normed_two_grad)
        totals["norm2_gain"] = totals["norm2_gain"] + gain2_part
        totals["norm2_bias"] = totals["norm2_bias"] + bias2_part
        hidden_grad = grad_rows.astype(jnp.float32) + hidden_part
        mixer_back = fetch_mixer(w_query, w_key, w_value, w_gate, w_output)
        query_back, key_back, value_back, gate_back_w, output_back = mixer_back
        hidden_grad_all = lax.all_gather(hidden_grad.astype(jnp.bfloat16), "tp", axis=0, tiled=True)
        totals["output"] = totals["output"] + row_product(gated_low, hidden_grad_all)
        gated_grad = back_product(hidden_grad_all, output_back)
        retained_grad, gate_pre_grad, gain_part, bias_part = gate_back(gated_grad)
        totals["group_gain"] = totals["group_gain"] + gain_part
        totals["group_bias"] = totals["group_bias"] + bias_part
        retained_grad_low = retained_grad.astype(jnp.bfloat16)
        gate_grad_low = gate_pre_grad.astype(jnp.bfloat16)

        def backward_block(running, block_id):
            key_acc, value_acc = running
            first_row = block_id * STRETCH
            query_tile_rows = lax.dynamic_slice_in_dim(query_low, first_row, STRETCH, 0)
            masking = decay_mask(first_row, segments, log_decay)
            retention_scores = jnp.einsum(
                "awx,bwx->wab", query_tile_rows, key_rounded, preferred_element_type=jnp.float32
            )
            weights_low = (retention_scores * masking * score_scale).astype(jnp.bfloat16)
            grad_block = lax.dynamic_slice_in_dim(retained_grad_low, first_row, STRETCH, 0)
            value_acc = value_acc + jnp.einsum(
                "hnm,nhe->mhe", weights_low, grad_block, preferred_element_type=jnp.float32
            )
            weight_grad = jnp.einsum(
                "nhe,mhe->hnm", grad_block, value_rounded, preferred_element_type=jnp.float32
            )
            score_gradient = (weight_grad * masking * score_scale).astype(jnp.bfloat16)
            query_grad = jnp.einsum(
                "geb,bgz->egz", score_gradient, key_rounded, preferred_element_type=jnp.float32
            )
            key_acc = key_acc + jnp.einsum(
                "sbe,bsg->esg", score_gradient, query_tile_rows, preferred_element_type=jnp.float32
            )
            return ((key_acc, value_acc), query_grad)

        starting = (
            jnp.zeros((length, heads_here, DK), jnp.float32),
            jnp.zeros((length, heads_here, DV), jnp.float32),
        )
        (key_rot_grad, value_grad), query_blocks = lax.scan(backward_block, starting, block_ids)
        query_rot_grad = query_blocks.reshape(length, heads_here, DK)
        query_grad_low = (
            rotate(query_rot_grad, position, -1.0).astype(jnp.bfloat16).reshape(length, query_cols)
        )
        key_grad_low = (
            rotate(key_rot_grad, position, -1.0).astype(jnp.bfloat16).reshape(length, query_cols)
        )
        value_grad_low = value_grad.astype(jnp.bfloat16).reshape(length, value_cols)
        totals["query"] = totals["query"] + row_product(normed_all, query_grad_low)
        totals["key"] = totals["key"] + row_product(normed_all, key_grad_low)
        totals["value"] = totals["value"] + row_product(normed_all, value_grad_low)
        totals["gate"] = totals["gate"] + row_product(normed_all, gate_grad_low)
        summed = back_product(query_grad_low, query_back)
        summed = summed + back_product(key_grad_low, key_back)
        summed = summed + back_product(value_grad_low, value_back)
        summed = summed + back_product(gate_grad_low, gate_back_w)
        normed_one_grad = lax.psum_scatter(
            summed.astype(jnp.bfloat16), "tp", scatter_dimension=0, tiled=True
        ).astype(jnp.float32)
        input_part, gain1_part, bias1_part = norm1_back(normed_one_grad)
        totals["norm1_gain"] = totals["norm1_gain"] + gain1_part
        totals["norm1_bias"] = totals["norm1_bias"] + bias1_part
        input_rows.append(hidden_grad + input_part)
    inner_shard = totals["inner"]
    outer_shard = totals["outer"]
    inner_bias_full = lax.dynamic_update_slice_in_dim(
        jnp.zeros(inner_all.shape, jnp.float32), totals["inner_bias"], tp_index * inner_cols, 0
    )
    weight_sums = (
        lax.psum_scatter(
            totals["query"].astype(jnp.bfloat16), "fsdp", scatter_dimension=0, tiled=True
        ).astype(jnp.float32),
        lax.psum_scatter(
            totals["key"].astype(jnp.bfloat16), "fsdp", scatter_dimension=0, tiled=True
        ).astype(jnp.float32),
        lax.psum_scatter(
            totals["value"].astype(jnp.bfloat16), "fsdp", scatter_dimension=0, tiled=True
        ).astype(jnp.float32),
        lax.psum_scatter(
            totals["gate"].astype(jnp.bfloat16), "fsdp", scatter_dimension=0, tiled=True
        ).astype(jnp.float32),
        lax.psum_scatter(
            totals["output"].astype(jnp.bfloat16), "fsdp", scatter_dimension=1, tiled=True
        ).astype(jnp.float32),
        lax.psum_scatter(
            inner_shard.astype(jnp.bfloat16), "fsdp", scatter_dimension=0, tiled=True
        ).astype(jnp.float32),
        lax.psum_scatter(
            outer_shard.astype(jnp.bfloat16), "fsdp", scatter_dimension=1, tiled=True
        ).astype(jnp.float32),
    )
    group_gain_full = lax.dynamic_update_slice_in_dim(
        jnp.zeros(group_gain_all.shape, jnp.float32), totals["group_gain"], tp_index * value_cols, 0
    )
    group_bias_full = lax.dynamic_update_slice_in_dim(
        jnp.zeros(group_bias_all.shape, jnp.float32), totals["group_bias"], tp_index * value_cols, 0
    )
    small_sums = (
        lax.psum_scatter(totals["norm1_gain"], ("fsdp", "tp"), scatter_dimension=0, tiled=True),
        lax.psum_scatter(totals["norm1_bias"], ("fsdp", "tp"), scatter_dimension=0, tiled=True),
        lax.psum_scatter(totals["norm2_gain"], ("fsdp", "tp"), scatter_dimension=0, tiled=True),
        lax.psum_scatter(totals["norm2_bias"], ("fsdp", "tp"), scatter_dimension=0, tiled=True),
        lax.psum_scatter(totals["outer_bias"], ("fsdp", "tp"), scatter_dimension=0, tiled=True),
        lax.psum_scatter(inner_bias_full, ("fsdp", "tp"), scatter_dimension=0, tiled=True),
        lax.psum_scatter(group_gain_full, ("fsdp", "tp"), scatter_dimension=0, tiled=True),
        lax.psum_scatter(group_bias_full, ("fsdp", "tp"), scatter_dimension=0, tiled=True),
    )
    out_stack = jnp.stack(out_rows)[:, None]
    input_stack = jnp.stack(input_rows)[:, None]
    return (
        out_stack,
        input_stack,
        small_sums[0],
        small_sums[1],
        weight_sums[0],
        weight_sums[1],
        weight_sums[2],
        weight_sums[3],
        weight_sums[4],
        small_sums[6],
        small_sums[7],
        small_sums[2],
        small_sums[3],
        weight_sums[5],
        small_sums[5],
        weight_sums[6],
        small_sums[4],
    )


def solution(mesh):
    placed = (
        P(None, "fsdp", "tp", None),
        P(None, "fsdp", None),
        P(("fsdp", "tp")),
        P(("fsdp", "tp")),
        P("fsdp", "tp"),
        P("fsdp", "tp"),
        P("fsdp", "tp"),
        P("fsdp", "tp"),
        P("tp", "fsdp"),
        P(("fsdp", "tp")),
        P(("fsdp", "tp")),
        P(("fsdp", "tp")),
        P(("fsdp", "tp")),
        P("fsdp", "tp"),
        P(("fsdp", "tp")),
        P("tp", "fsdp"),
        P(("fsdp", "tp")),
        P(None, "fsdp", "tp", None),
    )
    return jax.shard_map(
        shards,
        mesh=mesh,
        in_specs=placed,
        out_specs=(
            P(None, "fsdp", "tp", None),
            P(None, "fsdp", "tp", None),
            P(("fsdp", "tp")),
            P(("fsdp", "tp")),
            P("fsdp", "tp"),
            P("fsdp", "tp"),
            P("fsdp", "tp"),
            P("fsdp", "tp"),
            P("tp", "fsdp"),
            P(("fsdp", "tp")),
            P(("fsdp", "tp")),
            P(("fsdp", "tp")),
            P(("fsdp", "tp")),
            P("fsdp", "tp"),
            P(("fsdp", "tp")),
            P("tp", "fsdp"),
            P(("fsdp", "tp")),
        ),
        check_vma=False,
    )
```

profile of v0, /device:TPU:0, one launch (start us, length us, event | category | flops | bytes accessed | tf_op | source)
XLA Modules:
  0.0 2550.4 jit_solution(2416308836613303543)
XLA Ops:
  11.4 43.1 %all-reduce.14 = (f32[2048]{0:T(1024)S(1)}, f32[2048]{0:T(1024)S(1)}, f32[2048]{0:T(1024)}, f32[2048]{0:T(1024)}) all-reduce(f32[2048]{0:T(1024)S(1)} %dynamic-update-slice.1, f32[2048]{0:T(1024)S(1)} %dynamic-update-slice, f32[2048]{0:T(1024)S(1)} %dynamic-update-slice.3, ...), channel_id=1, replica_groups=mesh['fsdp'=8,'tp'=4] {'fsdp','tp'}, use_global_device_ids=true, to_apply=%add.1 | all-reduce | flops 8192 | bytes 65536
  66.0 68.6 %all-gather.2 = f32[32,1,128]{2,1,0:T(1,128)S(1)} all-gather(f32[1,1,128]{2,1,0:T(1,128)S(1)} %bitcast.497), channel_id=1, replica_groups=mesh['fsdp'=8,'tp'=4] {'fsdp','tp'}, dimensions={0}, use_global_device_ids=true | all-gather | bytes 16896 | tf_op jit(solution)/shard_map/all_gather | solution.py:128
  134.6 64.5 %all-gather.3 = f32[32,1,128]{2,1,0:T(1,128)S(1)} all-gather(f32[1,1,128]{2,1,0:T(1,128)S(1)} %bitcast.498), channel_id=1, replica_groups=mesh['fsdp'=8,'tp'=4] {'fsdp','tp'}, dimensions={0}, use_global_device_ids=true | all-gather | bytes 16896 | tf_op jit(solution)/shard_map/all_gather | solution.py:129
  199.1 9.8 fusion.125
  224.1 29.2 %all-gather.21.cloned.1.call-done = bf16[1024,2048]{1,0:T(8,128)(2,1)} async-done(((bf16[256,2048]{1,0:T(8,128)(2,1)}), bf16[1024,2048]{1,0:T(8,128)(2,1)}) %all-gather.21.cloned.1.call-update) | async-done | bytes 4194320 | tf_op jit(solution)/shard_map/all_gather | solution.py:175
  281.8 8.5 all-gather.29.cloned.1.call-done
  290.2 8.0 convolution_convert_fusion.2
  303.4 18.0 while.53
  321.4 7.3 copy.191
  340.3 7.2 convolution_convert_fusion.3
  352.6 17.3 while.52
  369.9 7.8 copy.182
  386.7 7.8 fusion.162
  396.5 12.5 multiply_convert_fusion.9
  408.9 10.7 fusion.161
  421.3 8.9 fusion.165
  431.0 133.5 %reduce-scatter.16.cloned.1.call-done = f32[256,2048]{1,0:T(8,128)} async-done(((f32[1024,2048]{1,0:T(8,128)}), f32[256,2048]{1,0:T(8,128)}) %reduce-scatter.16.cloned.1.call-update) | async-done | bytes 2097168 | tf_op jit(solution)/shard_map/reduce_scatter | solution.py:207
  564.6 147.6 %reduce-scatter.20.cloned.1.call-done = f32[256,2048]{1,0:T(8,128)} async-done(((f32[1024,2048]{1,0:T(8,128)}), f32[256,2048]{1,0:T(8,128)}) %reduce-scatter.20.cloned.1.call-update) | async-done | bytes 2097168 | tf_op jit(solution)/shard_map/reduce_scatter | solution.py:207
  721.4 68.7 %all-gather.4 = f32[32,1,128]{2,1,0:T(1,128)S(1)} all-gather(f32[1,1,128]{2,1,0:T(1,128)S(1)} %bitcast.499), channel_id=1, replica_groups=mesh['fsdp'=8,'tp'=4] {'fsdp','tp'}, dimensions={0}, use_global_device_ids=true | all-gather | bytes 16896 | tf_op jit(solution)/shard_map/all_gather | solution.py:127
  790.1 43.9 %all-gather.41.cloned.1.call-done = bf16[1024,2048]{1,0:T(8,128)(2,1)} async-done(((bf16[256,2048]{1,0:T(8,128)(2,1)}), bf16[1024,2048]{1,0:T(8,128)(2,1)}) %all-gather.41.cloned.1.call-update) | async-done | bytes 4194320 | tf_op jit(solution)/shard_map/all_gather | solution.py:218
  834.1 10.3 fusion.166
  844.4 71.0 %all-gather.33.cloned.1.call-done = bf16[1024,2048]{1,0:T(8,128)(2,1)} async-done(((bf16[256,2048]{1,0:T(8,128)(2,1)}), bf16[1024,2048]{1,0:T(8,128)(2,1)}) %all-gather.33.cloned.1.call-update) | async-done | bytes 4194320 | tf_op jit(solution)/shard_map/all_gather | solution.py:218
  915.4 27.2 %multiply_convert_fusion.8 = (bf16[1024,1024]{0,1:T(8,128)(2,1)}, f32[1024,1024]{0,1:T(8,128)}, bf16[1024,1024]{0,1:T(8,128)(2,1)}, f32[1024,1024]{0,1:T(8,128)}, f32[1024,1024]{0,1:T(8,128)}) fusion(f32[1024]{0:T(1024)S(1)} %dynamic_slice.54, f32[1024,1024]{0,1:T(8,128)} %fusion.166, bf16[1024,2048]{1,0:T(8,128)(2,1)} %all-gather.33.cloned.1.call-done, ...), kind=kOutput, calls=%fused_computation.138 | convolution fusion | flops 4433379328 | bytes 29364224 | tf_op jit(solution)/shard_map/dot_general | solution.py:220
  942.6 53.6 %all-gather.47.cloned.1.call-done = bf16[1,1,1024,2048]{3,2,1,0:T(8,128)(2,1)} async-done(((bf16[1,1,256,2048]{3,2,1,0:T(8,128)(2,1)}), bf16[1,1,1024,2048]{3,2,1,0:T(8,128)(2,1)}) %all-gather.47.cloned.1.call-update) | async-done | bytes 4194320 | tf_op jit(solution)/shard_map/all_gather | solution.py:239
  996.2 37.6 %all-gather.37.cloned.1.call-done = bf16[1024,2048]{1,0:T(8,128)(2,1)} async-done(((bf16[1024,256]{1,0:T(8,128)(2,1)}), bf16[1024,2048]{1,0:T(8,128)(2,1)}) %all-gather.37.cloned.1.call-update) | async-done | bytes 4194320 | tf_op jit(solution)/shard_map/all_gather | solution.py:90
  1033.8 12.0 convert_reduce_fusion.1
  1047.2 7.3 fusion.167
  1054.5 62.1 %all-gather.49.cloned.1.call-done = bf16[1,1,1024,2048]{3,2,1,0:T(8,128)(2,1)} async-done(((bf16[1,1,256,2048]{3,2,1,0:T(8,128)(2,1)}), bf16[1,1,1024,2048]{3,2,1,0:T(8,128)(2,1)}) %all-gather.49.cloned.1.call-update) | async-done | bytes 4194320 | tf_op jit(solution)/shard_map/all_gather | solution.py:239
  1116.6 12.0 convert_reduce_fusion
  1129.9 6.9 fusion.171
  1136.9 125.1 %reduce-scatter.24.cloned.1.call-done = f32[256,2048]{1,0:T(8,128)} async-done(((f32[1024,2048]{1,0:T(8,128)}), f32[256,2048]{1,0:T(8,128)}) %reduce-scatter.24.cloned.1.call-update) | async-done | bytes 2097168 | tf_op jit(solution)/shard_map/reduce_scatter | solution.py:247
  1261.9 147.5 %reduce-scatter.28.cloned.1.call-done = f32[256,2048]{1,0:T(8,128)} async-done(((f32[1024,2048]{1,0:T(8,128)}), f32[256,2048]{1,0:T(8,128)}) %reduce-scatter.28.cloned.1.call-update) | async-done | bytes 2097168 | tf_op jit(solution)/shard_map/reduce_scatter | solution.py:247
  1426.2 73.3 %all-gather.45.cloned.1.call-done = bf16[1024,2048]{1,0:T(8,128)(2,1)} async-done(((bf16[256,2048]{1,0:T(8,128)(2,1)}), bf16[1024,2048]{1,0:T(8,128)(2,1)}) %all-gather.45.cloned.1.call-update) | async-done | bytes 4194320 | tf_op jit(solution)/shard_map/all_gather | solution.py:256
  1499.5 14.1 fusion.140
  1513.6 67.3 %all-gather.43.cloned.1.call-done = bf16[1024,2048]{1,0:T(8,128)(2,1)} async-done(((bf16[256,2048]{1,0:T(8,128)(2,1)}), bf16[1024,2048]{1,0:T(8,128)(2,1)}) %all-gather.43.cloned.1.call-update) | async-done | bytes 4194320 | tf_op jit(solution)/shard_map/all_gather | solution.py:256
  1580.9 15.4 fusion.141
  1613.6 41.8 %while.55 = (s32[]{:T(128)}, f32[1024,2,256]{0,2,1:T(8,128)}, f32[1024,2,512]{0,2,1:T(8,128)}, f32[2,512,2,256]{3,1,0,2:T(8,128)}, s32[2]{0:T(128)S(1)}, /*index...) while((s32[]{:T(128)}, f32[1024,2,256]{0,2,1:T(8,128)}, ...), condition=%wide.region_40.41_spmd.clone, body=%wide.region_39.40_spmd.clone.sunk | while | flops 3775398400 | bytes 39340320 | solution.py:294
  1618.3 6.6 bitcast_add_fusion.11
  1637.7 8.0 bitcast_add_fusion.11
  1692.0 7.8 fusion.172
  1699.8 6.9 fusion.173
  1706.7 6.9 fusion.174
  1713.6 12.8 add_convert_fusion.5
  1728.0 38.4 %while.54 = (s32[]{:T(128)}, f32[1024,2,256]{0,2,1:T(8,128)S(1)}, f32[1024,2,512]{0,2,1:T(8,128)}, f32[2,512,2,256]{3,1,0,2:T(8,128)}, s32[2]{0:T(128)S(1)}, /*i...) while((s32[]{:T(128)}, f32[1024,2,256]{0,2,1:T(8,128)S(1)}, ...), condition=%wide.region_30.31_spmd.clone, body=%wide.region_29.30_spmd.clone.sunk | while | flops 3775398400 | bytes 39340320 | solution.py:294
  1732.6 6.8 bitcast_add_fusion.9
  1751.1 8.1 bitcast_add_fusion.9
  1782.2 7.1 fusion.169
  1789.3 6.9 fusion.170
  1796.2 11.2 add_convert_fusion.6
  1809.0 7.0 fusion.180
  1855.5 7.1 fusion.179
  1883.9 7.2 fusion.177
  1909.4 9.7 convolution_convert_fusion.1
  1919.2 9.4 convolution_convert_fusion
  1928.6 10.1 reduce-scatter.42.cloned.1.call-done
  1940.8 52.4 %reduce-scatter.44.cloned.1.call-done = bf16[1024,256]{1,0:T(8,128)(2,1)} async-done(((bf16[1024,2048]{1,0:T(8,128)(2,1)}), bf16[1024,256]{1,0:T(8,128)(2,1)}) %reduce-scatter.44.cloned.1.call-update) | async-done | bytes 524304 | tf_op jit(solution)/shard_map/reduce_scatter | solution.py:342
  1995.3 42.2 %reduce-scatter.34.cloned.1.call-done = bf16[256,512]{1,0:T(8,128)(2,1)} async-done(((bf16[2048,512]{1,0:T(8,128)(2,1)}), bf16[256,512]{1,0:T(8,128)(2,1)}) %reduce-scatter.34.cloned.1.call-update) | async-done | bytes 262160 | tf_op jit(solution)/shard_map/reduce_scatter | solution.py:327
  2039.3 42.6 %reduce-scatter.32.cloned.1.call-done = bf16[256,512]{1,0:T(8,128)(2,1)} async-done(((bf16[2048,512]{1,0:T(8,128)(2,1)}), bf16[256,512]{1,0:T(8,128)(2,1)}) %reduce-scatter.32.cloned.1.call-update) | async-done | bytes 262160 | tf_op jit(solution)/shard_map/reduce_scatter | solution.py:324
  2083.7 52.5 %reduce-scatter.40.cloned.1.call-done = bf16[1024,256]{1,0:T(8,128)(2,1)} async-done(((bf16[1024,2048]{1,0:T(8,128)(2,1)}), bf16[1024,256]{1,0:T(8,128)(2,1)}) %reduce-scatter.40.cloned.1.call-update) | async-done | bytes 524304 | tf_op jit(solution)/shard_map/reduce_scatter | solution.py:336
  2138.3 52.3 %reduce-scatter.38.cloned.1.call-done = bf16[256,1024]{1,0:T(8,128)(2,1)} async-done(((bf16[2048,1024]{1,0:T(8,128)(2,1)}), bf16[256,1024]{1,0:T(8,128)(2,1)}) %reduce-scatter.38.cloned.1.call-update) | async-done | bytes 524304 | tf_op jit(solution)/shard_map/reduce_scatter | solution.py:333
  2192.7 52.4 %reduce-scatter.36.cloned.1.call-done = bf16[256,1024]{1,0:T(8,128)(2,1)} async-done(((bf16[2048,1024]{1,0:T(8,128)(2,1)}), bf16[256,1024]{1,0:T(8,128)(2,1)}) %reduce-scatter.36.cloned.1.call-update) | async-done | bytes 524304 | tf_op jit(solution)/shard_map/reduce_scatter | solution.py:330
  2253.8 125.6 %all-reduce.17.cloned.1.call-done = (f32[2048]{0:T(1024)}, f32[2048]{0:T(1024)}, f32[2048]{0:T(1024)}, f32[4096]{0:T(1024)}, f32[4096]{0:T(1024)}, /*index=5*/f3...) async-done(((f32[2048]{0:T(1024)}, f32[2048]{0:T(1024)}, f32[2048]{0:T(1024)}, f32[4096]{0:T(1024)}, f32[4096]{0:T(1024)}, /*index=5*/f32[2048]{0:T(1024)}, ...) | async-done | bytes 98320
  2389.5 69.9 %reduce-scatter.18.cloned.1.call-done = bf16[256,2048]{1,0:T(8,128)(2,1)} async-done(((bf16[1024,2048]{1,0:T(8,128)(2,1)}), bf16[256,2048]{1,0:T(8,128)(2,1)}) %reduce-scatter.18.cloned.1.call-update) | async-done | bytes 1048592 | tf_op jit(solution)/shard_map/reduce_scatter | solution.py:226
  2459.4 79.6 %reduce-scatter.22.cloned.1.call-done = bf16[256,2048]{1,0:T(8,128)(2,1)} async-done(((bf16[1024,2048]{1,0:T(8,128)(2,1)}), bf16[256,2048]{1,0:T(8,128)(2,1)}) %reduce-scatter.22.cloned.1.call-update) | async-done | bytes 1048592 | tf_op jit(solution)/shard_map/reduce_scatter | solution.py:226
  (589 shorter events, 388.9 us)
Async XLA Ops:
  7.2 52.1 %copy-start.1 = (bf16[2,1,256,2048]{3,2,1,0:T(8,128)(2,1)S(1)}, bf16[2,1,256,2048]{3,2,1,0:T(8,128)(2,1)}, u32[]{:S(2)}) copy-start(bf16[2,1,256,2048]{3,2,1,0:T(8,128)(2,1)} %param.26) | copy-start | bytes 6291460
  7.2 201.8 %all-gather.25.cloned.1.call-start = ((), (), s32[]{:S(2)}) async-start(), calls=%async_computation.17 | async-start | bytes 2359296 | tf_op jit(solution)/shard_map/all_gather | solution.py:79
  7.9 201.1 %all-gather.39.cloned.1.call-start = ((), (), s32[]{:S(2)}) async-start(), calls=%async_computation.26 | async-start | bytes 5242880 | tf_op jit(solution)/shard_map/all_gather | solution.py:175
  58.7 75.9 %copy-start.119 = (f32[128]{0:T(128)S(1)}, f32[128]{0:T(128)}, u32[]{:S(2)}) copy-start(f32[128]{0:T(128)} %param.36) | copy-start | bytes 1540
  61.5 154.7 %all-gather.27.cloned.1.call-start = ((), (), s32[]{:S(2)}) async-start(), calls=%async_computation.18 | async-start | bytes 2359296 | tf_op jit(solution)/shard_map/all_gather | solution.py:80
  62.2 191.2 %all-gather.21.cloned.1.call-start = ((), (), s32[]{:S(2)}) async-start(), calls=%async_computation.15 | async-start | bytes 5242880 | tf_op jit(solution)/shard_map/all_gather | solution.py:175
  62.8 227.5 %all-gather.29.cloned.1.call-start = ((), (), s32[]{:S(2)}) async-start(), calls=%async_computation.19 | async-start | bytes 4718592 | tf_op jit(solution)/shard_map/all_gather | solution.py:81
  63.4 323.3 %all-gather.23.cloned.1.call-start = ((), (), s32[]{:S(2)}) async-start(), calls=%async_computation.16 | async-start | bytes 4718592 | tf_op jit(solution)/shard_map/all_gather | solution.py:82
  63.9 345.0 %all-gather.31.cloned.1.call-start = ((), (), s32[]{:S(2)}) async-start(), calls=%async_computation.20 | async-start | bytes 4718592 | tf_op jit(solution)/shard_map/all_gather | solution.py:83
  64.7 499.9 %reduce-scatter.16.cloned.1.call-start = ((), (), s32[]{:S(2)}) async-start(), calls=%async_computation.21 | async-start | bytes 10485760 | tf_op jit(solution)/shard_map/reduce_scatter | solution.py:207
  199.1 195.3 %copy-start.77 = (f32[1024]{0:T(1024)}, f32[1024]{0:T(1024)S(1)}, u32[]{:S(2)}) copy-start(f32[1024]{0:T(1024)S(1)} %dynamic_slice.52) | copy-start | bytes 12292
  199.1 195.3 %copy-start.87 = (f32[1024]{0:T(1024)}, f32[1024]{0:T(1024)S(1)}, u32[]{:S(2)}) copy-start(f32[1024]{0:T(1024)S(1)} %dynamic_slice.53) | copy-start | bytes 12292
  336.4 58.0 %copy-start.69 = (f32[2,512,2]{1,2,0:T(2,128)}, f32[2,512,2]{1,2,0:T(2,128)S(1)}, u32[]{:S(2)}) copy-start(f32[2,512,2]{1,2,0:T(2,128)S(1)} %broadcast_multiply_fusion.2) | copy-start | bytes 24580
  340.3 54.2 %copy-start.73 = (f32[1024,2]{0,1:T(2,128)}, f32[1024,2]{0,1:T(2,128)S(1)}, u32[]{:S(2)}) copy-start(f32[1024,2]{0,1:T(2,128)S(1)} %rsqrt.64) | copy-start | bytes 24580
  369.9 7.8 copy-start.13
  369.9 7.8 copy-start.61
  380.2 14.3 copy-start.67
  383.3 11.2 copy-start.71
  386.7 9.8 copy-start.16
  386.7 9.8 copy-start.17
  419.7 292.5 %reduce-scatter.20.cloned.1.call-start = ((), (), s32[]{:S(2)}) async-start(), calls=%async_computation.27 | async-start | bytes 10485760 | tf_op jit(solution)/shard_map/reduce_scatter | solution.py:207
  430.2 282.0 %copy-start.2 = (bf16[2,1,256,2048]{3,2,1,0:T(8,128)(2,1)S(1)}, bf16[2,1,256,2048]{3,2,1,0:T(8,128)(2,1)}, u32[]{:S(2)}) copy-start(bf16[2,1,256,2048]{3,2,1,0:T(8,128)(2,1)} %param.26) | copy-start | bytes 6291460
  430.2 359.9 %all-gather.35.cloned.1.call-start = ((), (), s32[]{:S(2)}) async-start(), calls=%async_computation.23 | async-start | bytes 4718592 | tf_op jit(solution)/shard_map/all_gather | solution.py:89
  430.8 403.2 %all-gather.41.cloned.1.call-start = ((), (), s32[]{:S(2)}) async-start(), calls=%async_computation.28 | async-start | bytes 5242880 | tf_op jit(solution)/shard_map/all_gather | solution.py:218
  717.9 197.6 %all-gather.33.cloned.1.call-start = ((), (), s32[]{:S(2)}) async-start(), calls=%async_computation.22 | async-start | bytes 5242880 | tf_op jit(solution)/shard_map/all_gather | solution.py:218
  718.4 277.8 %all-gather.47.cloned.1.call-start = ((), (), s32[]{:S(2)}) async-start(), calls=%async_computation.43 | async-start | bytes 5242880 | tf_op jit(solution)/shard_map/all_gather | solution.py:239
  720.2 313.6 %all-gather.37.cloned.1.call-start = ((), (), s32[]{:S(2)}) async-start(), calls=%async_computation.24 | async-start | bytes 4718592 | tf_op jit(solution)/shard_map/all_gather | solution.py:90
  720.8 395.8 %all-gather.49.cloned.1.call-start = ((), (), s32[]{:S(2)}) async-start(), calls=%async_computation.44 | async-start | bytes 5242880 | tf_op jit(solution)/shard_map/all_gather | solution.py:239
  721.4 540.6 %reduce-scatter.24.cloned.1.call-start = ((), (), s32[]{:S(2)}) async-start(), calls=%async_computation.30 | async-start | bytes 10485760 | tf_op jit(solution)/shard_map/reduce_scatter | solution.py:247
  1033.8 13.3 copy-start.129
  1054.5 354.9 %reduce-scatter.28.cloned.1.call-start = ((), (), s32[]{:S(2)}) async-start(), calls=%async_computation.33 | async-start | bytes 10485760 | tf_op jit(solution)/shard_map/reduce_scatter | solution.py:247
  1116.6 13.3 copy-start.130
  1136.8 272.6 %copy-start.5 = (f32[256,2048]{1,0:T(8,128)S(1)}, f32[256,2048]{1,0:T(8,128)}, u32[]{:S(2)}) copy-start(f32[256,2048]{1,0:T(8,128)} %copy-done.4) | copy-start | bytes 6291460
  1136.8 362.7 %all-gather.45.cloned.1.call-start = ((), (), s32[]{:S(2)}) async-start(), calls=%async_computation.34 | async-start | bytes 5242880 | tf_op jit(solution)/shard_map/all_gather | solution.py:256
  1418.0 162.9 %all-gather.43.cloned.1.call-start = ((), (), s32[]{:S(2)}) async-start(), calls=%async_computation.31 | async-start | bytes 5242880 | tf_op jit(solution)/shard_map/all_gather | solution.py:256
  1418.8 484.1 %reduce-scatter.30.cloned.1.call-start = ((), (), s32[]{:S(2)}) async-start(), calls=%async_computation.35 | async-start | bytes 5242880 | tf_op jit(solution)/shard_map/reduce_scatter | solution.py:311
  1423.8 75.7 %copy-start.70 = (f32[2,512,2]{1,2,0:T(2,128)S(1)}, f32[2,512,2]{1,2,0:T(2,128)}, u32[]{:S(2)}) copy-start(f32[2,512,2]{1,2,0:T(2,128)} %copy-done.69) | copy-start | bytes 24580
  1423.8 75.7 %copy-start.74 = (f32[1024,2]{0,1:T(2,128)S(1)}, f32[1024,2]{0,1:T(2,128)}, u32[]{:S(2)}) copy-start(f32[1024,2]{0,1:T(2,128)} %copy-done.73) | copy-start | bytes 24580
  1423.8 75.7 %copy-start.78 = (f32[1024]{0:T(1024)S(1)}, f32[1024]{0:T(1024)}, u32[]{:S(2)}) copy-start(f32[1024]{0:T(1024)} %copy-done.77) | copy-start | bytes 12292
  1423.8 75.7 %copy-start.88 = (f32[1024]{0:T(1024)S(1)}, f32[1024]{0:T(1024)}, u32[]{:S(2)}) copy-start(f32[1024]{0:T(1024)} %copy-done.87) | copy-start | bytes 12292
  1426.2 154.7 %copy-start.68 = (f32[2,512,2]{1,2,0:T(2,128)S(1)}, f32[2,512,2]{1,2,0:T(2,128)}, u32[]{:S(2)}) copy-start(f32[2,512,2]{1,2,0:T(2,128)} %copy-done.67) | copy-start | bytes 24580
  1426.2 154.7 %copy-start.72 = (f32[1024,2]{0,1:T(2,128)S(1)}, f32[1024,2]{0,1:T(2,128)}, u32[]{:S(2)}) copy-start(f32[1024,2]{0,1:T(2,128)} %copy-done.71) | copy-start | bytes 24580
  1686.7 26.9 %copy-start.37 = (bf16[1024,2,256]{0,2,1:T(8,128)(2,1)}, bf16[1024,2,256]{0,2,1:T(8,128)(2,1)S(1)}, u32[]{:S(2)}) copy-start(bf16[1024,2,256]{0,2,1:T(8,128)(2,1)S(1)} %copy.218) | copy-start | bytes 3145732
  1692.0 7.8 copy-start.56
  1692.0 7.8 copy-start.125
  1726.4 176.5 %reduce-scatter.26.cloned.1.call-start = ((), (), s32[]{:S(2)}) async-start(), calls=%async_computation.32 | async-start | bytes 5242880 | tf_op jit(solution)/shard_map/reduce_scatter | solution.py:311
  1807.5 131.2 %reduce-scatter.42.cloned.1.call-start = ((), (), s32[]{:S(2)}) async-start(), calls=%async_computation.41 | async-start | bytes 4718592 | tf_op jit(solution)/shard_map/reduce_scatter | solution.py:339
  1822.7 170.5 %reduce-scatter.44.cloned.1.call-start = ((), (), s32[]{:S(2)}) async-start(), calls=%async_computation.42 | async-start | bytes 4718592 | tf_op jit(solution)/shard_map/reduce_scatter | solution.py:342
  1836.8 200.7 %reduce-scatter.34.cloned.1.call-start = ((), (), s32[]{:S(2)}) async-start(), calls=%async_computation.37 | async-start | bytes 2359296 | tf_op jit(solution)/shard_map/reduce_scatter | solution.py:327
  1846.5 235.4 %reduce-scatter.32.cloned.1.call-start = ((), (), s32[]{:S(2)}) async-start(), calls=%async_computation.36 | async-start | bytes 2359296 | tf_op jit(solution)/shard_map/reduce_scatter | solution.py:324
  1855.2 281.0 %reduce-scatter.40.cloned.1.call-start = ((), (), s32[]{:S(2)}) async-start(), calls=%async_computation.40 | async-start | bytes 4718592 | tf_op jit(solution)/shard_map/reduce_scatter | solution.py:336
  1868.7 322.0 %reduce-scatter.38.cloned.1.call-start = ((), (), s32[]{:S(2)}) async-start(), calls=%async_computation.39 | async-start | bytes 4718592 | tf_op jit(solution)/shard_map/reduce_scatter | solution.py:333
  1883.4 361.7 %reduce-scatter.36.cloned.1.call-start = ((), (), s32[]{:S(2)}) async-start(), calls=%async_computation.38 | async-start | bytes 4718592 | tf_op jit(solution)/shard_map/reduce_scatter | solution.py:330
  1897.9 8.5 copy-start.114
  1897.9 8.5 copy-start.112
  1897.9 8.5 copy-start.102
  1897.9 8.5 copy-start.104
  1897.9 481.5 %all-reduce.17.cloned.1.call-start = ((), (), s32[]{:S(2)}) async-start(), calls=%async_computation.45 | async-start | bytes 196608
  1898.6 10.0 copy-start.97
  1909.2 550.2 %reduce-scatter.18.cloned.1.call-start = ((), (), s32[]{:S(2)}) async-start(), calls=%async_computation.25 | async-start | bytes 5242880 | tf_op jit(solution)/shard_map/reduce_scatter | solution.py:226
  1919.1 619.9 %reduce-scatter.22.cloned.1.call-start = ((), (), s32[]{:S(2)}) async-start(), calls=%async_computation.29 | async-start | bytes 5242880 | tf_op jit(solution)/shard_map/reduce_scatter | solution.py:226
  1940.8 306.5 %copy-start.108 = (f32[256]{0:T(256)S(1)}, f32[256]{0:T(256)}, u32[]{:S(2)}) copy-start(f32[256]{0:T(256)} %copy-done.107) | copy-start | bytes 3076
  1940.8 306.5 %copy-start.110 = (f32[256]{0:T(256)S(1)}, f32[256]{0:T(256)}, u32[]{:S(2)}) copy-start(f32[256]{0:T(256)} %copy-done.109) | copy-start | bytes 3076
  2251.5 287.5 %copy-start.6 = (f32[256,2048]{1,0:T(8,128)S(1)}, f32[256,2048]{1,0:T(8,128)}, u32[]{:S(2)}) copy-start(f32[256,2048]{1,0:T(8,128)} %copy-done.4) | copy-start | bytes 6291460
  (107 other events, 475.7 us)
Sparse Core Ops, SparseCore 0:
  9.9 30.6 all-gather.24
  61.6 80.6 all-gather.38
  144.2 26.3 all-gather.26
  172.6 80.7 all-gather.20
  255.1 35.0 all-gather.28
  292.0 36.5 all-gather.22
  330.5 37.3 all-gather.30
  419.8 144.7 reduce-scatter.15
  566.9 145.2 reduce-scatter.19
  713.9 37.2 all-gather.34
  753.3 80.6 all-gather.40
  836.1 79.2 all-gather.32
  917.0 79.2 all-gather.46
  998.0 35.8 all-gather.36
  1035.8 80.7 all-gather.48
  1118.8 143.0 reduce-scatter.23
  1264.1 145.2 reduce-scatter.27
  1418.1 81.3 all-gather.44
  1501.7 79.2 all-gather.42
  1726.5 75.2 reduce-scatter.29
  1807.6 76.0 reduce-scatter.25
  1887.0 51.6 reduce-scatter.41
  1942.1 51.0 reduce-scatter.43
  1996.3 41.1 reduce-scatter.33
  2040.8 41.1 reduce-scatter.31
  2085.1 51.0 reduce-scatter.39
  2139.4 51.1 reduce-scatter.37
  2194.0 51.1 reduce-scatter.35
  2252.2 127.1 all-reduce.16
  2381.5 77.8 reduce-scatter.17
  2461.7 77.2 reduce-scatter.21
where the time goes:
time: 2560 us; the launch traced here: 2550 us
  waiting for transfers between devices  1590 us (62%)
  matrix products  431 us (17%)
  blocking collectives  245 us (10%)
  other arithmetic  142 us (6%)
  local copies, waits for them, and re-layouts  121 us (5%)
    reduce_scatter x2, waiting for transfers between devices, shards(): lax.psum_scatter(jnp.dot(gated_low, output_full, preferred_element_type=j...  281 us
    reduce_scatter x2, waiting for transfers between devices, shards(): lax.psum_scatter(back_product(inner_grad_low, inner_back), 'tp', scatter_...  273 us
    reduce_scatter x2, waiting for transfers between devices, shards(): lax.psum_scatter(jnp.dot(active_low, outer_full, preferred_element_type=j...  150 us
    all_gather x2, waiting for transfers between devices, shards(): lax.all_gather(hidden_grad.astype(jnp.bfloat16), 'tp', axis=0, tiled=True)  141 us
    unnamed x32, waiting for transfers between devices  132 us
    dot_general x14, matrix products, back_product(): lax.dot_general(left, right, (((1,), (1,)), ((), ())), preferred_element_...  132 us
    all_gather x2, waiting for transfers between devices, shards(): grad_all = lax.all_gather(grad_rows, 'tp', axis=0, tiled=True)  116 us
    all_gather x2, waiting for transfers between devices, shards(): lax.all_gather(normed_two.astype(jnp.bfloat16), 'tp', axis=0, tiled=True)  115 us
  transfers between devices with their start and end apart: 31, of which 23 were waited for; matrix products, arithmetic and copies ran while one was open for 20% of the time, Pallas kernels for 0%

commit v1 on v0

v1 whole, which is shorter than its diff:
```python
import functools

import jax
import jax.numpy as jnp
from jax import lax
from jax.experimental import pallas as pl
from jax.experimental.pallas import tpu as pltpu
from jax.sharding import PartitionSpec as P

DK = 256
DV = 512
ROWS = 256

EPSILON = 1e-05
GROUP_EPSILON = 0.25
BF16 = jnp.bfloat16
F32 = jnp.float32


def layer_norm(values, scaling, offset):
    centred = values - jnp.mean(values, axis=-1, keepdims=True)
    variance = jnp.mean(centred * centred, axis=-1, keepdims=True)
    return centred * lax.rsqrt(variance + EPSILON) * scaling + offset


def doc_positions(segments):
    length = segments.shape[0]
    indices = jnp.arange(length, dtype=jnp.int32)
    previous = jnp.concatenate([jnp.full((1,), -1, jnp.int32), segments[:-1]])
    starts = lax.cummax(jnp.where(segments != previous, indices, 0), axis=0)
    return (indices - starts).astype(F32)


def dot_nn(left, right):
    return lax.dot_general(left, right, (((1,), (0,)), ((), ())), preferred_element_type=F32)


def dot_nt(left, right):
    return lax.dot_general(left, right, (((1,), (1,)), ((), ())), preferred_element_type=F32)


def dot_tn(left, right):
    return lax.dot_general(left, right, (((0,), (0,)), ((), ())), preferred_element_type=F32)


def turn(lead, trail, cosine, sinusoid):
    return jnp.concatenate(
        [lead * cosine - trail * sinusoid, lead * sinusoid + trail * cosine], axis=-1
    ).astype(BF16)


def mask_of(key_rows, key_cols, decay, length):
    gap = key_rows - key_cols
    inside = (gap >= 0.0) & (gap < length)
    return jnp.where(inside, jnp.exp(gap * decay), 0.0)


def retain_kernel(
    decay_ref, keyr_ref, keyc_ref, cos_ref, sin_ref, q_ref, k_ref, v_ref, g_ref, gain_ref, bias_ref, held_ref,
    gated_ref, kept_ref, qr_ref, kr_ref, vb_ref,
):
    del held_ref
    decay = decay_ref[pl.program_id(0)]
    length = q_ref.shape[0]
    half = DK // 2
    scale = DK ** (-0.5)
    qr_ref[...] = turn(q_ref[:, :half], q_ref[:, half:], cos_ref[...], sin_ref[...])
    kr_ref[...] = turn(k_ref[:, :half], k_ref[:, half:], cos_ref[...], sin_ref[...])
    vb_ref[...] = v_ref[...].astype(BF16)
    for first in range(0, length, ROWS):
        rows = pl.ds(first, ROWS)
        mask = mask_of(keyr_ref[rows, :], keyc_ref[...], decay, float(length))
        scores = dot_nt(qr_ref[rows, :], kr_ref[...])
        weights = (scores * mask * scale).astype(BF16)
        retained = dot_nn(weights, vb_ref[...])
        kept_ref[rows, :] = retained
        centred = retained - jnp.mean(retained, axis=-1, keepdims=True)
        variance = jnp.mean(centred * centred, axis=-1, keepdims=True)
        grouped = centred * lax.rsqrt(variance + GROUP_EPSILON) * gain_ref[...] + bias_ref[...]
        gate = g_ref[rows, :]
        gated_ref[rows, :] = (gate * jax.nn.sigmoid(gate) * grouped).astype(BF16)


def retain(decays, keyr, keyc, cosine, sinusoid, pre, gain, bias, held, place, heads):
    length = pre.shape[0]
    whole = lambda shape: pl.BlockSpec(shape, lambda h: (0,) * len(shape))
    cols = lambda width, start: pl.BlockSpec((length, width), lambda h: (0, start + h))
    vec = pl.BlockSpec((1, DV), lambda h: (0, h))
    return pl.pallas_call(
        retain_kernel,
        grid=(heads,),
        in_specs=[
            pl.BlockSpec(memory_space=pltpu.SMEM),
            whole((length, 1)), whole((1, length)),
            whole((length, DK // 2)), whole((length, DK // 2)),
            cols(DK, 0), cols(DK, heads), cols(DV, heads), cols(DV, 2 * heads),
            vec, vec,
            pl.BlockSpec(memory_space=pl.ANY),
        ],
        out_specs=[cols(DV, place * heads), cols(DV, 0), cols(DK, 0), cols(DK, 0), cols(DV, 0)],
        out_shape=[
            jax.ShapeDtypeStruct(held.shape, BF16),
            jax.ShapeDtypeStruct((length, heads * DV), F32),
            jax.ShapeDtypeStruct((length, heads * DK), BF16),
            jax.ShapeDtypeStruct((length, heads * DK), BF16),
            jax.ShapeDtypeStruct((length, heads * DV), BF16),
        ],
        input_output_aliases={11: 0},
        cost_estimate=pl.CostEstimate(
            flops=2 * heads * length * length * (DK + DV),
            bytes_accessed=heads * length * (2 * DK * 6 + DV * 16),
            transcendentals=heads * length * length,
        ),
        name="retain",
    )(decays, keyr, keyc, cosine, sinusoid, pre, pre, pre, pre, gain, bias, held)


def retain_back_kernel(
    decay_ref, keyr_ref, keyc_ref, cos_ref, sin_ref, qr_ref, kr_ref, vb_ref, g_ref, kept_ref, up_ref, gain_ref, bias_ref,
    grad_ref, dgain_ref, dbias_ref,
    dv_acc, dk_acc,
):
    head = pl.program_id(0)
    heads = pl.num_programs(0)
    decay = decay_ref[head]
    length = qr_ref.shape[0]
    half = DK // 2
    scale = DK ** (-0.5)
    at_q = pl.multiple_of(head * DK, DK)
    at_k = pl.multiple_of((heads + head) * DK, DK)
    at_v = pl.multiple_of((heads + head) * DV, DV)
    at_g = pl.multiple_of((2 * heads + head) * DV, DV)
    gain = gain_ref[...]
    bias = bias_ref[...]
    dgain = jnp.zeros((1, DV), F32)
    dbias = jnp.zeros((1, DV), F32)
    for first in range(0, length, ROWS):
        rows = pl.ds(first, ROWS)
        retained = kept_ref[rows, :]
        centred = retained - jnp.mean(retained, axis=-1, keepdims=True)
        variance = jnp.mean(centred * centred, axis=-1, keepdims=True)
        inverse = lax.rsqrt(variance + GROUP_EPSILON)
        unit = centred * inverse
        gate = g_ref[rows, :]
        open_gate = jax.nn.sigmoid(gate)
        up = up_ref[rows, :]
        grouped_grad = up * (gate * open_gate)
        gate_grad = up * (unit * gain + bias) * (open_gate * (1.0 + gate * (1.0 - open_gate)))
        grad_ref[rows, pl.ds(at_g, DV)] = gate_grad.astype(BF16)
        dgain = dgain + jnp.sum(grouped_grad * unit, axis=0, keepdims=True)
        dbias = dbias + jnp.sum(grouped_grad, axis=0, keepdims=True)
        unit_grad = grouped_grad * gain
        along = jnp.mean(unit_grad * unit, axis=-1, keepdims=True)
        level = jnp.mean(unit_grad, axis=-1, keepdims=True)
        retained_grad = (inverse * (unit_grad - level - unit * along)).astype(BF16)
        mask = mask_of(keyr_ref[rows, :], keyc_ref[...], decay, float(length)) * scale
        query = qr_ref[rows, :]
        weights = (dot_nt(query, kr_ref[...]) * mask).astype(BF16)
        value_part = dot_tn(weights, retained_grad)
        score_grad = (dot_nt(retained_grad, vb_ref[...]) * mask).astype(BF16)
        query_grad = dot_nn(score_grad, kr_ref[...])
        key_part = dot_tn(score_grad, query)
        if first == 0:
            dv_acc[...] = value_part
            dk_acc[...] = key_part
        else:
            dv_acc[...] += value_part
            dk_acc[...] += key_part
        grad_ref[rows, pl.ds(at_q, DK)] = turn(
            query_grad[:, :half], query_grad[:, half:], cos_ref[rows, :], -sin_ref[rows, :]
        )
    grad_ref[:, pl.ds(at_k, DK)] = turn(dk_acc[:, :half], dk_acc[:, half:], cos_ref[...], -sin_ref[...])
    grad_ref[:, pl.ds(at_v, DV)] = dv_acc[...].astype(BF16)
    dgain_ref[...] = dgain
    dbias_ref[...] = dbias


def retain_back(decays, keyr, keyc, cosine, sinusoid, qr, kr, vb, pre, kept, up, gain, bias, place, heads):
    length = pre.shape[0]
    whole = lambda shape: pl.BlockSpec(shape, lambda h: (0,) * len(shape))
    cols = lambda width, start: pl.BlockSpec((length, width), lambda h: (0, start + h))
    vec = pl.BlockSpec((1, DV), lambda h: (0, h))
    return pl.pallas_call(
        retain_back_kernel,
        grid=(heads,),
        in_specs=[
            pl.BlockSpec(memory_space=pltpu.SMEM),
            whole((length, 1)), whole((1, length)),
            whole((length, DK // 2)), whole((length, DK // 2)),
            cols(DK, 0), cols(DK, 0), cols(DV, 0), cols(DV, 2 * heads), cols(DV, 0), cols(DV, place * heads),
            vec, vec,
        ],
        out_specs=[whole((length, heads * 2 * (DK + DV))), vec, vec],
        out_shape=[
            jax.ShapeDtypeStruct((length, heads * 2 * (DK + DV)), BF16),
            jax.ShapeDtypeStruct((1, heads * DV), F32),
            jax.ShapeDtypeStruct((1, heads * DV), F32),
        ],
        scratch_shapes=[pltpu.VMEM((length, DV), F32), pltpu.VMEM((length, DK), F32)],
        cost_estimate=pl.CostEstimate(
            flops=2 * heads * length * length * (3 * DK + 2 * DV),
            bytes_accessed=heads * length * (2 * DK * 4 + DV * 18),
            transcendentals=heads * length * length,
        ),
        name="retain_back",
    )(decays, keyr, keyc, cosine, sinusoid, qr, kr, vb, pre, kept, up, gain, bias)


def shards(
    span, batches,
    tokens, segment, ln1_gain, ln1_bias, w_query, w_key, w_value, w_gate, w_output, gn_gain, gn_bias,
    ln2_gain, ln2_bias, w_inner, b_inner, w_outer, b_outer, cotangent,
):
    fsdp, tp = span
    teams = tp // batches
    devices = fsdp * tp
    place = lax.axis_index("tp")
    mine = place // teams
    rank = place % teams
    width = tokens.shape[3]
    piece = tokens.shape[2]
    heads = w_query.shape[1] // DK
    units = w_inner.shape[1]
    channels = w_value.shape[1]

    def along_team(value, shift):
        route = [
            (i, (i // teams) * teams + (i % teams + shift) % teams) for i in range(tp)
        ]
        return lax.ppermute(value, "tp", route)

    def across(value, shift):
        route = [
            (i, ((i // teams + shift) % batches) * teams + i % teams) for i in range(tp)
        ]
        return lax.ppermute(value, "tp", route)

    def quarter(back_batch, back_rank):
        return ((mine + batches - back_batch) % batches) * teams + (rank + teams - back_rank) % teams

    def pick(array, shift):
        return lax.dynamic_index_in_dim(array, (mine + shift) % batches, 0, keepdims=False)

    def own_rows(array):
        return jnp.concatenate(
            [pick(array, 0)[0]] + [across(pick(array, s)[0], s) for s in range(1, batches)], axis=0
        )

    def gather_team(value):
        return [value] + [along_team(value, s) for s in range(1, teams)]

    def scatter_team(part_of):
        sent = [along_team(part_of(s).astype(BF16), teams - s) for s in range(1, teams)]
        total = part_of(0)
        for received in sent:
            total = total + received.astype(F32)
        return total

    def give_back(rows):
        blocks = [rows[s * piece : (s + 1) * piece] for s in range(batches)]
        parts = [blocks[0]] + [
            across(blocks[s].astype(BF16), batches - s).astype(blocks[0].dtype) for s in range(1, batches)
        ]
        slots = []
        for i in range(batches):
            value = parts[0]
            for s in range(1, batches):
                value = jnp.where((mine + s) % batches == i, parts[s], value)
            slots.append(value)
        return jnp.stack(slots)[:, None]

    pieces = (ln1_gain, ln1_bias, ln2_gain, ln2_bias, b_outer, b_inner, gn_gain, gn_bias)
    flat = jnp.concatenate(pieces)
    used = flat.shape[0]
    lines = -(-used // 128)

    def exchange(table):
        padded = jnp.pad(table, ((0, 0), (0, lines * 128 - used))).reshape(devices, lines, 128)
        return lax.all_to_all(padded, ("fsdp", "tp"), 0, 0, tiled=True).reshape(devices, lines * 128)

    everyone = exchange(jnp.broadcast_to(flat[None], (devices, used)))
    vectors, begin = [], 0
    for item in pieces:
        vectors.append(everyone[:, begin : begin + item.shape[0]].reshape(-1))
        begin += item.shape[0]
    norm1_gain, norm1_bias, norm2_gain, norm2_bias, outer_bias, inner_all, group_gain_all, group_bias_all = vectors

    own_quarters = [quarter(s, 0) for s in range(batches)]

    def cut(vector, size):
        return [lax.dynamic_slice_in_dim(vector, q * size, size, 0) for q in own_quarters]

    inner_bias = jnp.concatenate(cut(inner_all, units))
    group_gains = [v[None] for v in cut(group_gain_all, channels)]
    group_biases = [v[None] for v in cut(group_bias_all, channels)]

    mixer_shard = jnp.concatenate([w_query, w_key, w_value, w_gate], axis=1)
    output_shard = w_output.T
    inner_shard = w_inner
    outer_shard = w_outer.T
    token_rows = own_rows(tokens)
    mixer_shards = [mixer_shard] + [across(mixer_shard, s) for s in range(1, batches)]
    mixers = [lax.all_gather(s, "fsdp", axis=0, tiled=True) for s in mixer_shards]

    def both(shard):
        return jnp.concatenate([shard] + [across(shard, s) for s in range(1, batches)], axis=1)

    output_full = lax.all_gather(both(output_shard), "fsdp", axis=0, tiled=True)
    inner_full = lax.all_gather(both(inner_shard), "fsdp", axis=0, tiled=True)
    outer_full = lax.all_gather(both(outer_shard), "fsdp", axis=0, tiled=True)
    grad_rows = own_rows(cotangent)
    grad_blocks = gather_team(grad_rows)

    segments = pick(segment, 0)[0]
    length = segments.shape[0]
    position = doc_positions(segments)
    order = [quarter(s, r) for r in range(teams) for s in range(batches)]

    def ordered(vector):
        return jnp.concatenate([lax.dynamic_slice_in_dim(vector, q * piece, piece, 0) for q in order])

    index = jnp.arange(length, dtype=jnp.int32)
    keys = ordered((segments * (2 * length) + index).astype(F32))
    keyr, keyc = keys[:, None], keys[None, :]
    frequency = 10000.0 ** (-jnp.arange(DK // 2, dtype=F32) / (DK // 2))
    angles = ordered(position)[:, None] * frequency[None, :]
    cosine, sinusoid = jnp.cos(angles), jnp.sin(angles)
    decays = [
        jnp.log1p(-(2.0 ** (-5.0 - (q * heads + jnp.arange(heads, dtype=jnp.int32)).astype(F32))))
        for q in own_quarters
    ]

    rows_in = token_rows.astype(F32)
    normed_one, norm1_back = jax.vjp(layer_norm, rows_in, norm1_gain, norm1_bias)
    normed_one_all = jnp.concatenate(gather_team(normed_one.astype(BF16)), axis=0)
    gated = jnp.zeros((length, batches * channels), BF16)
    saved = []
    for s in range(batches):
        pre = dot_nn(normed_one_all, mixers[s])
        gated, kept, qr, kr, vb = retain(
            decays[s], keyr, keyc, cosine, sinusoid, pre, group_gains[s], group_biases[s], gated, s, heads
        )
        saved.append((pre, kept, qr, kr, vb))
    block = batches * piece

    def rows_of(array, r):
        return array[r * block : (r + 1) * block]

    hidden = rows_in + scatter_team(lambda r: dot_nt(rows_of(gated, r), output_full))
    normed_two, norm2_back = jax.vjp(layer_norm, hidden, norm2_gain, norm2_bias)
    normed_two_blocks = gather_team(normed_two.astype(BF16))
    active_blocks, slope_blocks = [], []
    for normed in normed_two_blocks:
        inner = dot_nn(normed, inner_full) + inner_bias
        below = 0.5 * (1.0 + lax.erf(inner * (0.5**0.5)))
        active_blocks.append((inner * below).astype(BF16))
        bell = jnp.exp(-0.5 * inner * inner) * ((2.0 * jnp.pi) ** -0.5)
        slope_blocks.append((below + inner * bell).astype(BF16))

    inner_grad_blocks = [
        (slope.astype(F32) * dot_nn(grad, outer_full)).astype(BF16)
        for slope, grad in zip(slope_blocks, grad_blocks)
    ]
    normed_two_grad = scatter_team(lambda r: dot_nt(inner_grad_blocks[r], inner_full))
    hidden_part, norm2_gain_sum, norm2_bias_sum = norm2_back(normed_two_grad)
    hidden_grad = grad_rows.astype(F32) + hidden_part
    hidden_low_all = jnp.concatenate(gather_team(hidden_grad.astype(BF16)), axis=0)

    result = hidden + scatter_team(lambda r: dot_nt(active_blocks[r], outer_full)) + outer_bias
    out = give_back(result.astype(BF16))

    def reduce_columns(whole):
        return lax.psum_scatter(whole.astype(BF16), "fsdp", scatter_dimension=0, tiled=True)

    def settle(parts):
        total = parts[0].astype(F32)
        for s in range(1, batches):
            total = total + across(parts[s], batches - s).astype(F32)
        return total

    def settle_both(whole):
        size = whole.shape[1] // batches
        return settle([whole[:, s * size : (s + 1) * size] for s in range(batches)])

    active_all = jnp.concatenate(active_blocks, axis=0)
    grad_all = jnp.concatenate(grad_blocks, axis=0)
    inner_grad_all = jnp.concatenate(inner_grad_blocks, axis=0)
    normed_two_all = jnp.concatenate(normed_two_blocks, axis=0)
    grad_outer = settle_both(reduce_columns(dot_tn(grad_all, active_all))).T
    grad_inner = settle_both(reduce_columns(dot_tn(normed_two_all, inner_grad_all)))
    inner_bias_sum = jnp.sum(inner_grad_all.astype(F32), axis=0)
    outer_bias_sum = jnp.sum(grad_rows.astype(F32), axis=0)

    gated_grad = dot_nn(hidden_low_all, output_full)
    grads, gain_sums, bias_sums, mixer_sums = [], [], [], []
    for s in reversed(range(batches)):
        pre, kept, qr, kr, vb = saved[s]
        grad, gain_sum, bias_sum = retain_back(
            decays[s], keyr, keyc, cosine, sinusoid, qr, kr, vb, pre, kept, gated_grad,
            group_gains[s], group_biases[s], s, heads,
        )
        grads.insert(0, grad)
        gain_sums.insert(0, gain_sum[0])
        bias_sums.insert(0, bias_sum[0])
        mixer_sums.insert(0, reduce_columns(dot_tn(normed_one_all, grad)))
    grad_output = settle_both(reduce_columns(dot_tn(hidden_low_all, gated))).T

    def normed_one_part(r):
        total = dot_nt(rows_of(grads[0], r), mixers[0])
        for s in range(1, batches):
            total = total + dot_nt(rows_of(grads[s], r), mixers[s])
        return total

    normed_one_grad = scatter_team(normed_one_part)
    input_part, norm1_gain_sum, norm1_bias_sum = norm1_back(normed_one_grad)
    input_grad = give_back(hidden_grad + input_part)
    grad_mixer = settle(mixer_sums)
    narrow, wide = w_query.shape[1], channels
    grad_query = grad_mixer[:, :narrow]
    grad_key = grad_mixer[:, narrow : 2 * narrow]
    grad_value = grad_mixer[:, 2 * narrow : 2 * narrow + wide]
    grad_gate = grad_mixer[:, 2 * narrow + wide :]

    def spread(parts, size):
        total = jnp.zeros((tp * size,), F32)
        for q, part in zip(own_quarters, parts):
            total = lax.dynamic_update_slice_in_dim(total, part, q * size, 0)
        return total

    sums = (
        norm1_gain_sum,
        norm1_bias_sum,
        norm2_gain_sum,
        norm2_bias_sum,
        outer_bias_sum,
        spread([inner_bias_sum[s * units : (s + 1) * units] for s in range(batches)], units),
        spread(gain_sums, channels),
        spread(bias_sums, channels),
    )
    shared = jnp.sum(exchange(jnp.concatenate([v.reshape(devices, -1) for v in sums], axis=1)), axis=0)
    small, begin = [], 0
    for item in pieces:
        small.append(shared[begin : begin + item.shape[0]])
        begin += item.shape[0]
    return (
        out, input_grad, small[0], small[1], grad_query, grad_key, grad_value, grad_gate, grad_output,
        small[6], small[7], small[2], small[3], grad_inner, small[5], grad_outer, small[4],
    )


def solution(mesh):
    rows, vec = P(None, "fsdp", "tp", None), P(("fsdp", "tp"))
    tall, flat = P("fsdp", "tp"), P("tp", "fsdp")
    span = (mesh.shape["fsdp"], mesh.shape["tp"])

    def step(*args):
        return jax.shard_map(
            functools.partial(shards, span, args[0].shape[0]),
            mesh=mesh,
            in_specs=(
                rows, P(None, "fsdp", None), vec, vec, tall, tall, tall, tall, flat,
                vec, vec, vec, vec, tall, vec, flat, vec, rows,
            ),
            out_specs=(
                rows, rows, vec, vec, tall, tall, tall, tall, flat,
                vec, vec, vec, vec, tall, vec, flat, vec,
            ),
            check_vma=False,
        )(*args)

    return step
```

time: 2560 us -> 1120 us (0.44)
  waiting for transfers between devices: 1590 us -> 626 us
  blocking collectives: 245 us -> 0 us
  matrix products: 431 us -> 285 us
  other arithmetic: 142 us -> 45.3 us
  local copies, waits for them, and re-layouts: 121 us -> 35.9 us
  Pallas kernels: 0 us -> 68.8 us
  starting transfers between devices: 2.38 us -> 35.4 us
    reduce_scatter x15 -> x5, waiting for transfers between devices: 1010 us -> 0.01 us  [reduce_columns(): lax.psum_scatter(whole.astype(BF16), 'fsdp', scatter_dimension=0, tiled=T...]
    ppermute x0 -> x20, waiting for transfers between devices: none -> 533 us  [the longest x8 298 us: along_team(): return lax.ppermute(value, 'tp', route)]
    all_gather x15 -> x5, waiting for transfers between devices: 447 us -> 0.05 us  [the longest x2 0.02 us: shards(): lax.all_gather(s, 'fsdp', axis=0, tiled=True)]
    all_gather x3 -> x0, blocking collectives: 202 us -> none  [the longest x1 68.7 us: shards(): lax.all_gather(b_inner, ('fsdp', 'tp'), axis=0, tiled=True)]
    dot_general x62 -> x22, matrix products: 431 us -> 285 us  [the longest x10 111 us: dot_nt(): lax.dot_general(left, right, (((1,), (1,)), ((), ())), preferred_element_...]
    unnamed x32 -> x10, waiting for transfers between devices: 132 us -> 0.16 us
    all_to_all x0 -> x2, waiting for transfers between devices: none -> 92.8 us  [exchange(): lax.all_to_all(padded, ('fsdp', 'tp'), 0, 0, tiled=True)]
    pallas_call x0 -> x4, Pallas kernels: none -> 68.8 us  [the longest x2 43.2 us: retain_back(): pl.pallas_call(retain_back_kernel, grid=(heads,), in_specs=[pl.BlockSpec(...]
  transfers between devices with their start and end apart: 31 -> 32, of which waited for: 23 -> 16; matrix products, arithmetic and copies ran while one was open for 20% -> 30% of each run, Pallas kernels for 0% -> 6%
where the time goes in v1:
time: 1120 us; the launch traced here: 1110 us
  waiting for transfers between devices  626 us (56%)
  matrix products  285 us (25%)
  Pallas kernels  68.8 us (6%)
  other arithmetic  45.3 us (4%)
  local copies, waits for them, and re-layouts  35.9 us (3%)
  starting transfers between devices  35.4 us (3%)
  between operations  15.5 us (1%)
    ppermute x8, waiting for transfers between devices, along_team(): return lax.ppermute(value, 'tp', route)  298 us
    ppermute x12, waiting for transfers between devices, across(): return lax.ppermute(value, 'tp', route)  234 us
    dot_general x10, matrix products, dot_nt(): lax.dot_general(left, right, (((1,), (1,)), ((), ())), preferred_element_...  111 us
    all_to_all x2, waiting for transfers between devices, exchange(): lax.all_to_all(padded, ('fsdp', 'tp'), 0, 0, tiled=True)  92.8 us
    dot_general x7, matrix products, dot_nn(): lax.dot_general(left, right, (((1,), (0,)), ((), ())), preferred_element_...  90.8 us
    dot_general x5, matrix products, dot_tn(): lax.dot_general(left, right, (((0,), (0,)), ((), ())), preferred_element_...  83.3 us
    pallas_call x2, Pallas kernels, retain_back(): pl.pallas_call(retain_back_kernel, grid=(heads,), in_specs=[pl.BlockSpec(...  43.2 us
    pallas_call x2, Pallas kernels, retain(): pl.pallas_call(retain_kernel, grid=(heads,), in_specs=[pl.BlockSpec(memor...  25.6 us
  transfers between devices with their start and end apart: 32, of which 16 were waited for; matrix products, arithmetic and copies ran while one was open for 30% of the time, Pallas kernels for 6%

profile of v1, /device:TPU:0, one launch (start us, length us, event | category | flops | bytes accessed | tf_op | source)
XLA Modules:
  0.0 1111.8 jit_solution(504342668807578443)
XLA Ops:
  12.6 4.1 collective-permute-start.2
  16.7 68.4 %collective-permute-done.2 = bf16[256,3072]{1,0:T(8,128)(2,1)} collective-permute-done((bf16[256,3072]{1,0:T(8,128)(2,1)}, bf16[256,3072]{1,0:T(8,128)(2,1)}, u32[]{:S(2)}, u32[]{:S(2)}) %collective-permute-start.2) | collective-permute-done | bytes 1572896 | tf_op jit(solution)/shard_map/ppermute | solution.py:236
  85.3 25.4 %collective-permute-done.3 = bf16[256,1024]{0,1:T(8,128)(2,1)S(1)} collective-permute-done((bf16[256,1024]{0,1:T(8,128)(2,1)}, bf16[256,1024]{0,1:T(8,128)(2,1)S(1)}, u32[]{:S(2)}, u32[]{:S(2)}) %collective-permute-start.3) | collective-permute-done | bytes 524320 | tf_op jit(solution)/shard_map/ppermute | solution.py:236
  110.7 2.1 pad_maximum_fusion.8
  113.0 24.6 %collective-permute-done.5 = bf16[256,1024]{1,0:T(8,128)(2,1)S(1)} collective-permute-done((bf16[256,1024]{1,0:T(8,128)(2,1)}, bf16[256,1024]{1,0:T(8,128)(2,1)S(1)}, u32[]{:S(2)}, u32[]{:S(2)}) %collective-permute-start.5) | collective-permute-done | bytes 524320 | tf_op jit(solution)/shard_map/ppermute | solution.py:236
  137.6 2.2 pad_maximum_fusion.9
  142.1 4.5 all-to-all-start
  146.6 2.7 collective-permute-start.6
  149.8 53.2 %all-to-all-done = f32[32,6,128]{2,1,0:T(8,128)S(1)} async-done(((f32[32,6,128]{2,1,0:T(8,128)}), f32[32,6,128]{2,1,0:T(8,128)S(1)}, u32[]{:S(2)}, u32[]{:S(2)}) %all-to-all-start) | async-done | bytes 98336 | tf_op jit(solution)/shard_map/all_to_all | solution.py:279
  205.4 2.2 fusion.7
  210.7 3.0 multiply_sine_fusion
  217.2 41.4 %collective-permute-done.1 = bf16[512,2048]{1,0:T(8,128)(2,1)} collective-permute-done((bf16[512,2048]{1,0:T(8,128)(2,1)}, bf16[512,2048]{1,0:T(8,128)(2,1)}, u32[]{:S(2)}, u32[]{:S(2)}) %collective-permute-start.1) | collective-permute-done | bytes 2097184 | tf_op jit(solution)/shard_map/ppermute | solution.py:230
  258.6 19.2 %fusion.58.q_ref.k_ref.v_ref.g_ref = f32[1024,3072]{1,0:T(8,128)} fusion(bf16[2048,3072]{1,0:T(8,128)(2,1)} %all-gather.8.cloned.1.call-done, bf16[512,2048]{1,0:T(8,128)(2,1)} %collective-permute-done.1, bf16[512,2048]{1,0:T(8,128)(2,1)} %fusion.7), kind=kOutput, calls=%fused_computation.145 | convolution fusion | flops 12893290496 | bytes 29360128 | tf_op jit(solution)/shard_map/dot_general | solution.py:35
  277.7 2.5 broadcast_in_dim.62.held_ref
  280.3 12.7 %retain.2 = (bf16[1024,2048]{1,0:T(8,128)(2,1)}, f32[1024,1024]{1,0:T(8,128)}, bf16[1024,512]{1,0:T(8,128)(2,1)}, bf16[1024,512]{1,0:T(8,128)(2,1)}, bf16[1024,1024]{1,0:T(8,128)(2,1)}) custom-call(f32[2]{0:T(128)} %negate_log-plus-one_fusion.decay_ref, f32[1024,1]{1,0:T(8,128)} %copy.42.keyr_ref, ...), custom_call_target="tpu_custom_call", output_to_operand_aliasing={{0}: (11, {})} | custom-call | flops 3221225472 | bytes 23068672 | tf_op jit(solution)/shard_map/retain/pallas_call | solution.py:89
  293.0 19.0 %fusion.59.q_ref.k_ref.v_ref.g_ref = f32[1024,3072]{1,0:T(8,128)} fusion(bf16[2048,3072]{1,0:T(8,128)(2,1)} %all-gather.6.cloned.1.call-done, bf16[512,2048]{1,0:T(8,128)(2,1)} %collective-permute-done.1, bf16[512,2048]{1,0:T(8,128)(2,1)} %fusion.7), kind=kOutput, calls=%fused_computation.146 | convolution fusion | flops 12893290496 | bytes 29360128 | tf_op jit(solution)/shard_map/dot_general | solution.py:35
  312.0 12.9 %retain.3 = (bf16[1024,2048]{1,0:T(8,128)(2,1)}, f32[1024,1024]{1,0:T(8,128)}, bf16[1024,512]{1,0:T(8,128)(2,1)}, bf16[1024,512]{1,0:T(8,128)(2,1)}, bf16[1024,1024]{1,0:T(8,128)(2,1)}) custom-call(f32[2]{0:T(128)} %negate_log-plus-one_fusion.1.decay_ref, f32[1024,1]{1,0:T(8,128)} %copy.42.keyr_ref, ...), custom_call_target="tpu_custom_call", output_to_operand_aliasing={{0}: (11, {})} | custom-call | flops 3221225472 | bytes 23068672 | tf_op jit(solution)/shard_map/retain/pallas_call | solution.py:89
  324.9 10.0 convolution_convert_fusion.7
  336.0 3.1 collective-permute-start.10
  339.2 65.9 %collective-permute-done.4 = bf16[512,2048]{1,0:T(8,128)(2,1)} collective-permute-done((bf16[512,2048]{1,0:T(8,128)(2,1)}, bf16[512,2048]{1,0:T(8,128)(2,1)}, u32[]{:S(2)}, u32[]{:S(2)}) %collective-permute-start.4) | collective-permute-done | bytes 2097184 | tf_op jit(solution)/shard_map/ppermute | solution.py:230
  405.1 9.4 fusion.73
  415.1 2.2 add_convert_fusion.2
  418.7 2.1 collective-permute-start.11
  420.8 45.3 %collective-permute-done.7 = bf16[512,2048]{1,0:T(8,128)(2,1)} collective-permute-done((bf16[512,2048]{1,0:T(8,128)(2,1)}, bf16[512,2048]{1,0:T(8,128)(2,1)}, u32[]{:S(2)}, u32[]{:S(2)}) %collective-permute-start.7) | collective-permute-done | bytes 2097184 | tf_op jit(solution)/shard_map/ppermute | solution.py:230
  466.1 10.6 fusion.74
  476.7 32.5 %collective-permute-done.11 = bf16[512,2048]{1,0:T(8,128)(2,1)} collective-permute-done((bf16[512,2048]{1,0:T(8,128)(2,1)S(1)}, bf16[512,2048]{1,0:T(8,128)(2,1)}, u32[]{:S(2)}, u32[]{:S(2)}) %collective-permute-start.11) | collective-permute-done | bytes 2097184 | tf_op jit(solution)/shard_map/ppermute | solution.py:230
  509.2 9.5 multiply_convert_fusion
  518.7 9.3 convolution_convert_fusion.5
  528.3 8.8 multiply_convert_fusion.3
  539.1 13.2 %convolution_convert_fusion.2 = bf16[2048,2048]{1,0:T(8,128)(2,1)} fusion(bf16[512,2048]{1,0:T(8,128)(2,1)} %collective-permute-done.11, bf16[256,2048]{1,0:T(8,128)(2,1)} %collective-permute-done.10, bf16[256,2048]{1,0:T(8,128)(2,1)S(1)} %get-tuple-element.104, bf16[512,2048]{1,0:T(8,128)(2,1)S(1)} %get-tuple-element.123, ...), kind=kOutput, calls=%fused_computation.3 | convolution fusion | flops 8615100416 | bytes 16777216 | tf_op jit(solution)/shard_map/dot_general | solution.py:43
  552.4 9.6 multiply_convert_fusion.1
  562.0 12.2 %collective-permute-done.12 = bf16[512,2048]{1,0:T(8,128)(2,1)} collective-permute-done((bf16[512,2048]{1,0:T(8,128)(2,1)}, bf16[512,2048]{1,0:T(8,128)(2,1)}, u32[]{:S(2)}, u32[]{:S(2)}) %collective-permute-start.12) | collective-permute-done | bytes 2097184 | tf_op jit(solution)/shard_map/ppermute | solution.py:230
  574.1 10.1 multiply_reduce_fusion
  585.4 3.5 convert_reduce_fusion.2
  589.3 44.4 %collective-permute-done.13 = bf16[512,2048]{1,0:T(8,128)(2,1)S(1)} collective-permute-done((bf16[512,2048]{1,0:T(8,128)(2,1)S(1)}, bf16[512,2048]{1,0:T(8,128)(2,1)S(1)}, u32[]{:S(2)}, u32[]{:S(2)}) %collective-permute-start.13) | collective-permute-done | bytes 2097184 | tf_op jit(solution)/shard_map/ppermute | solution.py:230
  633.7 14.2 %fusion.44.up_ref = f32[1024,2048]{1,0:T(8,128)} fusion(bf16[2048,2048]{0,1:T(8,128)(2,1)} %all-gather.10.cloned.1.call-done, bf16[512,2048]{1,0:T(8,128)(2,1)S(1)} %collective-permute-done.13, bf16[512,2048]{1,0:T(8,128)(2,1)S(1)} %get-tuple-element.103), kind=kOutput, calls=%fused_computation.78 | convolution fusion | flops 8598323200 | bytes 20971520 | tf_op jit(solution)/shard_map/dot_general | solution.py:35
  648.0 21.7 %retain_back.3 = (bf16[1024,3072]{1,0:T(8,128)(2,1)}, f32[1,1024]{1,0:T(1,128)}, f32[1,1024]{1,0:T(1,128)}) custom-call(f32[2]{0:T(128)} %negate_log-plus-one_fusion.1.decay_ref, f32[1024,1]{1,0:T(8,128)} %copy.42.keyr_ref, f32[1,1024]{1,0:T(1,128)} %bitcast.106, f32[1024,128]{1,0:T(8,128)} %get-tuple-element.125.cos_ref, ...), custom_call_target="tpu_custom_call" | custom-call | flops 7516192768 | bytes 23068672 | tf_op jit(solution)/shard_map/retain_back/pallas_call | solution.py:183
  669.6 19.9 %convolution_convert_fusion = bf16[2048,3072]{1,0:T(8,128)(2,1)} fusion(bf16[1024,3072]{1,0:T(8,128)(2,1)} %get-tuple-element.44, bf16[512,2048]{1,0:T(8,128)(2,1)} %collective-permute-done.1, bf16[512,2048]{1,0:T(8,128)(2,1)} %fusion.7), kind=kOutput, calls=%fused_computation | convolution fusion | flops 12899581952 | bytes 23068672 | tf_op jit(solution)/shard_map/dot_general | solution.py:43
  689.6 14.0 %convolution_convert_fusion.3 = bf16[2048,2048]{1,0:T(8,128)(2,1)} fusion(bf16[512,2048]{1,0:T(8,128)(2,1)} %collective-permute-done.7, bf16[512,2048]{1,0:T(8,128)(2,1)} %add_convert_fusion.2, bf16[512,2048]{1,0:T(8,128)(2,1)S(1)} %multiply_convert_fusion, bf16[512,2048]{1,0:T(8,128)(2,1)} %copy-done.16), kind=kOutput, calls=%fused_computation.4 | convolution fusion | flops 8610906112 | bytes 16777216 | tf_op jit(solution)/shard_map/dot_general | solution.py:43
  703.6 16.2 %convolution_convert_fusion.4 = bf16[2048,2048]{1,0:T(8,128)(2,1)} fusion(bf16[1024,2048]{1,0:T(8,128)(2,1)} %get-tuple-element.34, bf16[512,2048]{1,0:T(8,128)(2,1)} %copy-done.52, bf16[512,2048]{1,0:T(8,128)(2,1)} %copy-done.18), kind=kOutput, calls=%fused_computation.5 | convolution fusion | flops 8602517504 | bytes 16777216 | tf_op jit(solution)/shard_map/dot_general | solution.py:43
  719.9 21.5 %retain_back.2 = (bf16[1024,3072]{1,0:T(8,128)(2,1)}, f32[1,1024]{1,0:T(1,128)}, f32[1,1024]{1,0:T(1,128)}) custom-call(f32[2]{0:T(128)} %negate_log-plus-one_fusion.decay_ref, f32[1024,1]{1,0:T(8,128)} %copy.42.keyr_ref, f32[1,1024]{1,0:T(1,128)} %bitcast.107, f32[1024,128]{1,0:T(8,128)} %get-tuple-element.125.cos_ref, ...), custom_call_target="tpu_custom_call" | custom-call | flops 7516192768 | bytes 23068672 | tf_op jit(solution)/shard_map/retain_back/pallas_call | solution.py:183
  741.5 20.1 %convolution_convert_fusion.1 = bf16[2048,3072]{1,0:T(8,128)(2,1)} fusion(bf16[1024,3072]{1,0:T(8,128)(2,1)} %get-tuple-element.39, bf16[512,2048]{1,0:T(8,128)(2,1)} %collective-permute-done.1, bf16[512,2048]{1,0:T(8,128)(2,1)} %fusion.7), kind=kOutput, calls=%fused_computation.1 | convolution fusion | flops 12899581952 | bytes 23068672 | tf_op jit(solution)/shard_map/dot_general | solution.py:43
  762.4 10.0 convolution_convert_fusion.6
  774.2 12.2 %fusion.34 = f32[512,2048]{1,0:T(8,128)} fusion(bf16[2048,3072]{1,0:T(8,128)(2,1)} %all-gather.8.cloned.1.call-done, bf16[1024,3072]{1,0:T(8,128)(2,1)} %get-tuple-element.39), kind=kOutput, calls=%fused_computation.69 | convolution fusion | flops 6442450944 | bytes 19922944 | tf_op jit(solution)/shard_map/dot_general | solution.py:39
  786.4 14.4 %add_convert_fusion = bf16[512,2048]{1,0:T(8,128)(2,1)} fusion(f32[512,2048]{1,0:T(8,128)} %fusion.34, bf16[2048,3072]{1,0:T(8,128)(2,1)} %all-gather.6.cloned.1.call-done, bf16[1024,3072]{1,0:T(8,128)(2,1)} %get-tuple-element.44), kind=kOutput, calls=%fused_computation.54 | convolution fusion | flops 6444548096 | bytes 22020096 | tf_op jit(solution)/shard_map/dot_general | solution.py:39
  801.9 19.3 %collective-permute-done.8 = bf16[512,2048]{1,0:T(8,128)(2,1)} collective-permute-done((bf16[512,2048]{1,0:T(8,128)(2,1)}, bf16[512,2048]{1,0:T(8,128)(2,1)}, u32[]{:S(2)}, u32[]{:S(2)}) %collective-permute-start.8) | collective-permute-done | bytes 2097184 | tf_op jit(solution)/shard_map/ppermute | solution.py:230
  821.2 10.9 add_convert_fusion.1
  833.7 2.5 collective-permute-start.9
  836.1 12.2 %fusion.38 = f32[512,2048]{1,0:T(8,128)} fusion(bf16[2048,3072]{1,0:T(8,128)(2,1)} %all-gather.8.cloned.1.call-done, bf16[1024,3072]{1,0:T(8,128)(2,1)} %get-tuple-element.39), kind=kOutput, calls=%fused_computation.73 | convolution fusion | flops 6442450944 | bytes 19922944 | tf_op jit(solution)/shard_map/dot_general | solution.py:39
  848.3 37.4 %collective-permute-done.14 = bf16[512,2048]{1,0:T(8,128)(2,1)} collective-permute-done((bf16[512,2048]{1,0:T(8,128)(2,1)}, bf16[512,2048]{1,0:T(8,128)(2,1)}, u32[]{:S(2)}, u32[]{:S(2)}) %collective-permute-start.14) | collective-permute-done | bytes 2097184 | tf_op jit(solution)/shard_map/ppermute | solution.py:230
  885.7 12.7 %fusion.61 = (f32[2048]{0:T(1024)S(1)}, f32[512]{0:T(512)S(1)}, f32[512,2048]{1,0:T(8,128)S(1)}) fusion(f32[2048]{0:T(1024)S(1)} %copy-done.25, f32[512]{0:T(512)S(1)} %copy-done.28, bf16[256,2048]{1,0:T(8,128)(2,1)S(1)} %copy-done.8, bf16[256,2048]{1,0:T(8,128)(2,1)S(1)} %copy-done.3, bf16[512,2048]{1,0:T(8,128)(2,1)} %collective-permute-done.14, ...), kind=kOutput, calls=%fused_computation.148 | convolution fusion | flops 6455031296 | bytes 28332032 | tf_op jit(solution)/shard_map/dot_general | solution.py:39
  898.5 2.6 fusion.8
  901.2 3.4 add_add_fusion.2
  910.6 4.1 all-to-all-start.1
  916.2 39.5 %all-to-all-done.1 = f32[32,6,128]{2,1,0:T(8,128)S(1)} async-done(((f32[32,6,128]{2,1,0:T(8,128)}), f32[32,6,128]{2,1,0:T(8,128)S(1)}, u32[]{:S(2)}, u32[]{:S(2)}) %all-to-all-start.1) | async-done | bytes 98336 | tf_op jit(solution)/shard_map/all_to_all | solution.py:279
  959.6 2.2 collective-permute-start.16
  961.8 3.8 fusion.46
  968.3 4.1 maximum_bitcast_fusion
  974.4 2.1 collective-permute-start.17
  976.5 65.2 %collective-permute-done.19 = bf16[256,1024]{1,0:T(8,128)(2,1)} collective-permute-done((bf16[256,1024]{1,0:T(8,128)(2,1)}, bf16[256,1024]{1,0:T(8,128)(2,1)}, u32[]{:S(2)}, u32[]{:S(2)}) %collective-permute-start.19) | collective-permute-done | bytes 524320 | tf_op jit(solution)/shard_map/ppermute | solution.py:236
  1044.2 42.4 %collective-permute-done.18 = bf16[256,1024]{1,0:T(8,128)(2,1)} collective-permute-done((bf16[256,1024]{1,0:T(8,128)(2,1)}, bf16[256,1024]{1,0:T(8,128)(2,1)}, u32[]{:S(2)}, u32[]{:S(2)}) %collective-permute-start.18) | collective-permute-done | bytes 524320 | tf_op jit(solution)/shard_map/ppermute | solution.py:236
  1086.6 2.2 convert_add_fusion.5
  1088.8 8.3 collective-permute-done.17
  1099.6 2.4 convert_add_fusion.4
  (245 shorter events, 53.5 us)
Async XLA Ops:
  7.2 251.4 %all-gather.8.cloned.1.call-start = ((), (), s32[]{:S(2)}) async-start(), calls=%async_computation.8 | async-start | bytes 14155776 | tf_op jit(solution)/shard_map/all_gather | solution.py:303
  12.5 127.3 %copy-start.13 = (bf16[2,1,256,2048]{3,2,1,0:T(8,128)(2,1)S(1)}, bf16[2,1,256,2048]{3,2,1,0:T(8,128)(2,1)}, u32[]{:S(2)}) copy-start(bf16[2,1,256,2048]{3,2,1,0:T(8,128)(2,1)} %param.18) | copy-start | bytes 6291460
  12.5 280.4 %all-gather.6.cloned.1.call-start = ((), (), s32[]{:S(2)}) async-start(), calls=%async_computation.7 | async-start | bytes 14155776 | tf_op jit(solution)/shard_map/all_gather | solution.py:303
  12.6 72.5 %collective-permute-start.2 = (bf16[256,3072]{1,0:T(8,128)(2,1)}, bf16[256,3072]{1,0:T(8,128)(2,1)}, u32[]{:S(2)}, u32[]{:S(2)}) collective-permute-start(bf16[256,3072]{1,0:T(8,128)(2,1)} %copy-done.12), channel_id=1, source_target_pairs={{0,2},{1,3},{2,0},{3,1},{4,6},{5,7},{6,4},{7,5},{8,10},{9,11},{10,... | collective-permute-start | bytes 4718600 | tf_op jit(solution)/shard_map/ppermute | solution.py:236
  85.2 239.7 %all-gather.10.cloned.1.call-start = ((), (), s32[]{:S(2)}) async-start(), calls=%async_computation.9 | async-start | bytes 9437184 | tf_op jit(solution)/shard_map/all_gather | solution.py:308
  85.2 25.5 %collective-permute-start.3 = (bf16[256,1024]{0,1:T(8,128)(2,1)}, bf16[256,1024]{0,1:T(8,128)(2,1)S(1)}, u32[]{:S(2)}, u32[]{:S(2)}) collective-permute-start(bf16[256,1024]{0,1:T(8,128)(2,1)} %bitcast.99), channel_id=1, source_target_pairs={{0,2},{1,3},{2,0},{3,1},{4,6},{5,7},{6,4},{7,5},{8,10},{9,11},{10,... | collective-permute-start | bytes 1572872 | tf_op jit(solution)/shard_map/ppermute | solution.py:236
  112.8 28.2 %copy-start.43 = (f32[64]{0:T(128)S(1)}, f32[64]{0:T(128)}, u32[]{:S(2)}) copy-start(f32[64]{0:T(128)} %param.20) | copy-start | bytes 772
  112.8 28.2 %copy-start.44 = (f32[64]{0:T(128)S(1)}, f32[64]{0:T(128)}, u32[]{:S(2)}) copy-start(f32[64]{0:T(128)} %param.21) | copy-start | bytes 772
  112.8 28.2 %copy-start.45 = (f32[64]{0:T(128)S(1)}, f32[64]{0:T(128)}, u32[]{:S(2)}) copy-start(f32[64]{0:T(128)} %param.29) | copy-start | bytes 772
  112.8 28.2 %copy-start.46 = (f32[64]{0:T(128)S(1)}, f32[64]{0:T(128)}, u32[]{:S(2)}) copy-start(f32[64]{0:T(128)} %param.30) | copy-start | bytes 772
  112.8 28.2 %copy-start.47 = (f32[64]{0:T(128)S(1)}, f32[64]{0:T(128)}, u32[]{:S(2)}) copy-start(f32[64]{0:T(128)} %param.34) | copy-start | bytes 772
  112.8 28.2 %copy-start.48 = (f32[128]{0:T(128)S(1)}, f32[128]{0:T(128)}, u32[]{:S(2)}) copy-start(f32[128]{0:T(128)} %param.32) | copy-start | bytes 1540
  112.8 28.2 %copy-start.49 = (f32[128]{0:T(128)S(1)}, f32[128]{0:T(128)}, u32[]{:S(2)}) copy-start(f32[128]{0:T(128)} %param.27) | copy-start | bytes 1540
  112.8 28.2 %copy-start.50 = (f32[128]{0:T(128)S(1)}, f32[128]{0:T(128)}, u32[]{:S(2)}) copy-start(f32[128]{0:T(128)} %param.28) | copy-start | bytes 1540
  112.9 36.5 %copy-start.38 = (s32[2,1,1024]{2,1,0:T(1,128)S(1)}, s32[2,1,1024]{2,1,0:T(1,128)}, u32[]{:S(2)}) copy-start(s32[2,1,1024]{2,1,0:T(1,128)} %param.19) | copy-start | bytes 24580
  112.9 307.9 %all-gather.12.cloned.1.call-start = ((), (), s32[]{:S(2)}) async-start(), calls=%async_computation.10 | async-start | bytes 9437184 | tf_op jit(solution)/shard_map/all_gather | solution.py:309
  112.9 24.7 %collective-permute-start.5 = (bf16[256,1024]{1,0:T(8,128)(2,1)}, bf16[256,1024]{1,0:T(8,128)(2,1)S(1)}, u32[]{:S(2)}, u32[]{:S(2)}) collective-permute-start(bf16[256,1024]{1,0:T(8,128)(2,1)} %param.31), channel_id=1, source_target_pairs={{0,2},{1,3},{2,0},{3,1},{4,6},{5,7},{6,4},{7,5},{8,10},{9,11},{10,... | collective-permute-start | bytes 1572872 | tf_op jit(solution)/shard_map/ppermute | solution.py:236
  141.0 264.1 %copy-start.2 = (bf16[256,2048]{1,0:T(8,128)(2,1)}, bf16[256,2048]{1,0:T(8,128)(2,1)S(1)}, u32[]{:S(2)}) copy-start(bf16[256,2048]{1,0:T(8,128)(2,1)S(1)} %get-tuple-element.106) | copy-start | bytes 3145732
  141.0 62.8 %collective-permute-start = (bf16[256,2048]{1,0:T(8,128)(2,1)}, bf16[256,2048]{1,0:T(8,128)(2,1)S(1)}, u32[]{:S(2)}, u32[]{:S(2)}) collective-permute-start(bf16[256,2048]{1,0:T(8,128)(2,1)} %get-tuple-element.107), channel_id=1, source_target_pairs={{0,2},{1,3},{2,0},{3,1},{4,6},{5,7},{6,4},{7,5},{8,10},{9,11},{10,... | collective-permute-start | bytes 3145736 | tf_op jit(solution)/shard_map/ppermute | solution.py:236
  142.1 61.0 %all-to-all-start = ((f32[32,6,128]{2,1,0:T(8,128)}), f32[32,6,128]{2,1,0:T(8,128)S(1)}, u32[]{:S(2)}, u32[]{:S(2)}) async-start(f32[32,6,128]{2,1,0:T(8,128)} %pad.13), calls=%async_computation | async-start | bytes 262144 | tf_op jit(solution)/shard_map/all_to_all | solution.py:279
  146.5 362.7 %all-gather.14.cloned.1.call-start = ((), (), s32[]{:S(2)}) async-start(), calls=%async_computation.11 | async-start | bytes 9437184 | tf_op jit(solution)/shard_map/all_gather | solution.py:310
  146.6 68.9 %collective-permute-start.6 = (bf16[256,1024]{0,1:T(8,128)(2,1)}, bf16[256,1024]{0,1:T(8,128)(2,1)S(1)}, u32[]{:S(2)}, u32[]{:S(2)}) collective-permute-start(bf16[256,1024]{0,1:T(8,128)(2,1)} %bitcast.101), channel_id=1, source_target_pairs={{0,2},{1,3},{2,0},{3,1},{4,6},{5,7},{6,4},{7,5},{8,10},{9,11},{10,... | collective-permute-start | bytes 1572872 | tf_op jit(solution)/shard_map/ppermute | solution.py:236
  203.8 201.3 %copy-start.7 = (bf16[256,2048]{1,0:T(8,128)(2,1)}, bf16[256,2048]{1,0:T(8,128)(2,1)S(1)}, u32[]{:S(2)}) copy-start(bf16[256,2048]{1,0:T(8,128)(2,1)S(1)} %collective-permute-done) | copy-start | bytes 3145732
  204.2 11.4 %copy-start.22 = (bf16[1024,256]{1,0:T(8,128)(2,1)S(1)}, bf16[1024,256]{1,0:T(8,128)(2,1)}, u32[]{:S(2)}) copy-start(bf16[1024,256]{1,0:T(8,128)(2,1)} %param.33) | copy-start | bytes 1572868
  207.6 50.9 %collective-permute-start.1 = (bf16[512,2048]{1,0:T(8,128)(2,1)}, bf16[512,2048]{1,0:T(8,128)(2,1)}, u32[]{:S(2)}, u32[]{:S(2)}) collective-permute-start(bf16[512,2048]{1,0:T(8,128)(2,1)} %fusion.7), channel_id=1, source_target_pairs={{0,1},{1,0},{2,3},{3,2},{4,5},{5,4},{6,7},{7,6},{8,9},{9,8},{10,11... | collective-permute-start | bytes 6291464 | tf_op jit(solution)/shard_map/ppermute | solution.py:230
  209.1 68.6 %copy-start.23 = (f32[1024]{0:T(1024)}, f32[1024]{0:T(1024)S(1)}, u32[]{:S(2)}) copy-start(f32[1024]{0:T(1024)S(1)} %pad_maximum_fusion.12) | copy-start | bytes 12292
  216.6 740.3 %reduce-scatter.14.cloned.1.call-start = ((), (), s32[]{:S(2)}) async-start(), calls=%async_computation.16 | async-start | bytes 9437184 | tf_op jit(solution)/shard_map/reduce_scatter | solution.py:373
  334.9 70.3 %collective-permute-start.4 = (bf16[512,2048]{1,0:T(8,128)(2,1)}, bf16[512,2048]{1,0:T(8,128)(2,1)}, u32[]{:S(2)}, u32[]{:S(2)}) collective-permute-start(bf16[512,2048]{1,0:T(8,128)(2,1)} %convolution_convert_fusion.7), channel_id=1, source_target_pairs={{0,1},{1,0},{2,3},{3,2},{4,5},{5,4},{6,7},{7,6},{8,9},{9,8},{10,11... | collective-permute-start | bytes 6291464 | tf_op jit(solution)/shard_map/ppermute | solution.py:230
  336.0 249.4 %copy-start.9 = (bf16[256,2048]{1,0:T(8,128)(2,1)}, bf16[256,2048]{1,0:T(8,128)(2,1)S(1)}, u32[]{:S(2)}) copy-start(bf16[256,2048]{1,0:T(8,128)(2,1)S(1)} %get-tuple-element.104) | copy-start | bytes 3145732
  336.0 81.3 %collective-permute-start.10 = (bf16[256,2048]{1,0:T(8,128)(2,1)}, bf16[256,2048]{1,0:T(8,128)(2,1)}, u32[]{:S(2)}, u32[]{:S(2)}) collective-permute-start(bf16[256,2048]{1,0:T(8,128)(2,1)} %get-tuple-element.105), channel_id=1, source_target_pairs={{0,2},{1,3},{2,0},{3,1},{4,6},{5,7},{6,4},{7,5},{8,10},{9,11},{10,... | collective-permute-start | bytes 3145736 | tf_op jit(solution)/shard_map/ppermute | solution.py:236
  417.3 48.8 %collective-permute-start.7 = (bf16[512,2048]{1,0:T(8,128)(2,1)}, bf16[512,2048]{1,0:T(8,128)(2,1)}, u32[]{:S(2)}, u32[]{:S(2)}) collective-permute-start(bf16[512,2048]{1,0:T(8,128)(2,1)} %add_convert_fusion.2), channel_id=1, source_target_pairs={{0,1},{1,0},{2,3},{3,2},{4,5},{5,4},{6,7},{7,6},{8,9},{9,8},{10,11... | collective-permute-start | bytes 6291464 | tf_op jit(solution)/shard_map/ppermute | solution.py:230
  418.7 90.5 %collective-permute-start.11 = (bf16[512,2048]{1,0:T(8,128)(2,1)S(1)}, bf16[512,2048]{1,0:T(8,128)(2,1)}, u32[]{:S(2)}, u32[]{:S(2)}) collective-permute-start(bf16[512,2048]{1,0:T(8,128)(2,1)S(1)} %pad_maximum_fusion.7), channel_id=1, source_target_pairs={{0,1},{1,0},{2,3},{3,2},{4,5},{5,4},{6,7},{7,6},{8,9},{9,8},{10,11... | collective-permute-start | bytes 6291464 | tf_op jit(solution)/shard_map/ppermute | solution.py:230
  528.0 46.1 %collective-permute-start.12 = (bf16[512,2048]{1,0:T(8,128)(2,1)}, bf16[512,2048]{1,0:T(8,128)(2,1)}, u32[]{:S(2)}, u32[]{:S(2)}) collective-permute-start(bf16[512,2048]{1,0:T(8,128)(2,1)} %convolution_convert_fusion.5), channel_id=1, source_target_pairs={{0,1},{1,0},{2,3},{3,2},{4,5},{5,4},{6,7},{7,6},{8,9},{9,8},{10,11... | collective-permute-start | bytes 6291464 | tf_op jit(solution)/shard_map/ppermute | solution.py:230
  552.3 407.3 %reduce-scatter.8.cloned.1.call-start = ((), (), s32[]{:S(2)}) async-start(), calls=%async_computation.13 | async-start | bytes 14155776 | tf_op jit(solution)/shard_map/reduce_scatter | solution.py:373
  552.4 21.8 %copy-start.5 = (f32[512,2048]{1,0:T(8,128)S(1)}, f32[512,2048]{1,0:T(8,128)}, u32[]{:S(2)}) copy-start(f32[512,2048]{1,0:T(8,128)} %copy-done.4) | copy-start | bytes 12582916
  562.0 22.2 %copy-start.16 = (bf16[512,2048]{1,0:T(8,128)(2,1)}, bf16[512,2048]{1,0:T(8,128)(2,1)S(1)}, u32[]{:S(2)}) copy-start(bf16[512,2048]{1,0:T(8,128)(2,1)S(1)} %multiply_convert_fusion.1) | copy-start | bytes 6291460
  588.9 59.1 %copy-start.18 = (bf16[512,2048]{1,0:T(8,128)(2,1)}, bf16[512,2048]{1,0:T(8,128)(2,1)S(1)}, u32[]{:S(2)}) copy-start(bf16[512,2048]{1,0:T(8,128)(2,1)S(1)} %get-tuple-element.103) | copy-start | bytes 6291460
  588.9 44.8 %collective-permute-start.13 = (bf16[512,2048]{1,0:T(8,128)(2,1)S(1)}, bf16[512,2048]{1,0:T(8,128)(2,1)S(1)}, u32[]{:S(2)}, u32[]{:S(2)}) collective-permute-start(bf16[512,2048]{1,0:T(8,128)(2,1)S(1)} %get-tuple-element.103), channel_id=1, source_target_pairs={{0,1},{1,0},{2,3},{3,2},{4,5},{5,4},{6,7},{7,6},{8,9},{9,8},{10,11... | collective-permute-start | bytes 6291464 | tf_op jit(solution)/shard_map/ppermute | solution.py:230
  633.7 14.2 %copy-start.52 = (bf16[512,2048]{1,0:T(8,128)(2,1)}, bf16[512,2048]{1,0:T(8,128)(2,1)S(1)}, u32[]{:S(2)}) copy-start(bf16[512,2048]{1,0:T(8,128)(2,1)S(1)} %collective-permute-done.13) | copy-start | bytes 6291460
  689.5 276.0 %reduce-scatter.12.cloned.1.call-start = ((), (), s32[]{:S(2)}) async-start(), calls=%async_computation.15 | async-start | bytes 9437184 | tf_op jit(solution)/shard_map/reduce_scatter | solution.py:373
  703.6 268.8 %reduce-scatter.10.cloned.1.call-start = ((), (), s32[]{:S(2)}) async-start(), calls=%async_computation.14 | async-start | bytes 9437184 | tf_op jit(solution)/shard_map/reduce_scatter | solution.py:373
  719.9 379.7 %reduce-scatter.6.cloned.1.call-start = ((), (), s32[]{:S(2)}) async-start(), calls=%async_computation.12 | async-start | bytes 14155776 | tf_op jit(solution)/shard_map/reduce_scatter | solution.py:373
  772.4 48.8 %collective-permute-start.8 = (bf16[512,2048]{1,0:T(8,128)(2,1)}, bf16[512,2048]{1,0:T(8,128)(2,1)}, u32[]{:S(2)}, u32[]{:S(2)}) collective-permute-start(bf16[512,2048]{1,0:T(8,128)(2,1)} %convolution_convert_fusion.6), channel_id=1, source_target_pairs={{0,1},{1,0},{2,3},{3,2},{4,5},{5,4},{6,7},{7,6},{8,9},{9,8},{10,11... | collective-permute-start | bytes 6291464 | tf_op jit(solution)/shard_map/ppermute | solution.py:230
  786.4 34.8 %copy-start.6 = (f32[512,2048]{1,0:T(8,128)S(1)}, f32[512,2048]{1,0:T(8,128)}, u32[]{:S(2)}) copy-start(f32[512,2048]{1,0:T(8,128)} %copy-done.4) | copy-start | bytes 12582916
  800.8 31.3 %copy-start.37 = (f32[2048]{0:T(1024)S(1)}, f32[2048]{0:T(1024)}, u32[]{:S(2)}) copy-start(f32[2048]{0:T(1024)} %get-tuple-element.83) | copy-start | bytes 24580
  800.8 31.4 %copy-start.36 = (f32[2048]{0:T(1024)S(1)}, f32[2048]{0:T(1024)}, u32[]{:S(2)}) copy-start(f32[2048]{0:T(1024)} %get-tuple-element.87) | copy-start | bytes 24580
  800.8 31.5 %copy-start.31 = (f32[2048]{0:T(1024)S(1)}, f32[2048]{0:T(1024)}, u32[]{:S(2)}) copy-start(f32[2048]{0:T(1024)} %get-tuple-element.102) | copy-start | bytes 24580
  800.8 84.9 %collective-permute-start.14 = (bf16[512,2048]{1,0:T(8,128)(2,1)}, bf16[512,2048]{1,0:T(8,128)(2,1)}, u32[]{:S(2)}, u32[]{:S(2)}) collective-permute-start(bf16[512,2048]{1,0:T(8,128)(2,1)} %add_convert_fusion), channel_id=1, source_target_pairs={{0,1},{1,0},{2,3},{3,2},{4,5},{5,4},{6,7},{7,6},{8,9},{9,8},{10,11... | collective-permute-start | bytes 6291464 | tf_op jit(solution)/shard_map/ppermute | solution.py:230
  833.6 52.1 %copy-start.3 = (bf16[256,2048]{1,0:T(8,128)(2,1)S(1)}, bf16[256,2048]{1,0:T(8,128)(2,1)}, u32[]{:S(2)}) copy-start(bf16[256,2048]{1,0:T(8,128)(2,1)} %copy-done.2) | copy-start | bytes 3145732
  833.6 52.1 %copy-start.8 = (bf16[256,2048]{1,0:T(8,128)(2,1)S(1)}, bf16[256,2048]{1,0:T(8,128)(2,1)}, u32[]{:S(2)}) copy-start(bf16[256,2048]{1,0:T(8,128)(2,1)} %copy-done.7) | copy-start | bytes 3145732
  833.7 52.1 %copy-start.25 = (f32[2048]{0:T(1024)S(1)}, f32[2048]{0:T(1024)}, u32[]{:S(2)}) copy-start(f32[2048]{0:T(1024)} %copy-done.24) | copy-start | bytes 24580
  833.7 52.0 %copy-start.28 = (f32[512]{0:T(512)S(1)}, f32[512]{0:T(512)}, u32[]{:S(2)}) copy-start(f32[512]{0:T(512)} %copy-done.27) | copy-start | bytes 6148
  833.7 74.6 %collective-permute-start.9 = (bf16[256,2048]{1,0:T(8,128)(2,1)S(1)}, bf16[256,2048]{1,0:T(8,128)(2,1)S(1)}, u32[]{:S(2)}, u32[]{:S(2)}) collective-permute-start(bf16[256,2048]{1,0:T(8,128)(2,1)S(1)} %slice.179), channel_id=1, source_target_pairs={{0,2},{1,3},{2,0},{3,1},{4,6},{5,7},{6,4},{7,5},{8,10},{9,11},{10,... | collective-permute-start | bytes 3145736 | tf_op jit(solution)/shard_map/ppermute | solution.py:236
  848.3 50.1 %copy-start.33 = (f32[512]{0:T(512)S(1)}, f32[512]{0:T(512)}, u32[]{:S(2)}) copy-start(f32[512]{0:T(512)} %copy-done.32) | copy-start | bytes 6148
  848.3 50.2 %copy-start.30 = (f32[512]{0:T(512)S(1)}, f32[512]{0:T(512)}, u32[]{:S(2)}) copy-start(f32[512]{0:T(512)} %copy-done.29) | copy-start | bytes 6148
  906.8 55.0 %collective-permute-start.15 = (bf16[256,2048]{1,0:T(8,128)(2,1)S(1)}, bf16[256,2048]{1,0:T(8,128)(2,1)}, u32[]{:S(2)}, u32[]{:S(2)}) collective-permute-start(bf16[256,2048]{1,0:T(8,128)(2,1)S(1)} %slice.225), channel_id=1, source_target_pairs={{0,2},{1,3},{2,0},{3,1},{4,6},{5,7},{6,4},{7,5},{8,10},{9,11},{10,... | collective-permute-start | bytes 3145736 | tf_op jit(solution)/shard_map/ppermute | solution.py:236
  910.6 45.2 %all-to-all-start.1 = ((f32[32,6,128]{2,1,0:T(8,128)}), f32[32,6,128]{2,1,0:T(8,128)S(1)}, u32[]{:S(2)}, u32[]{:S(2)}) async-start(f32[32,6,128]{2,1,0:T(8,128)} %reshape.195), calls=%async_computation.1 | async-start | bytes 262144 | tf_op jit(solution)/shard_map/all_to_all | solution.py:279
  958.8 82.8 %collective-permute-start.19 = (bf16[256,1024]{1,0:T(8,128)(2,1)}, bf16[256,1024]{1,0:T(8,128)(2,1)}, u32[]{:S(2)}, u32[]{:S(2)}) collective-permute-start(bf16[256,1024]{1,0:T(8,128)(2,1)} %slice.194), channel_id=1, source_target_pairs={{0,2},{1,3},{2,0},{3,1},{4,6},{5,7},{6,4},{7,5},{8,10},{9,11},{10,... | collective-permute-start | bytes 1572872 | tf_op jit(solution)/shard_map/ppermute | solution.py:236
  959.6 140.0 %collective-permute-start.16 = (bf16[256,3072]{1,0:T(8,128)(2,1)}, bf16[256,3072]{1,0:T(8,128)(2,1)}, u32[]{:S(2)}, u32[]{:S(2)}) collective-permute-start(bf16[256,3072]{1,0:T(8,128)(2,1)} %reduce-scatter.8.cloned.1.call-done), channel_id=1, source_target_pairs={{0,2},{1,3},{2,0},{3,1},{4,6},{5,7},{6,4},{7,5},{8,10},{9,11},{10,... | collective-permute-start | bytes 4718600 | tf_op jit(solution)/shard_map/ppermute | solution.py:236
  967.4 119.1 %collective-permute-start.18 = (bf16[256,1024]{1,0:T(8,128)(2,1)}, bf16[256,1024]{1,0:T(8,128)(2,1)}, u32[]{:S(2)}, u32[]{:S(2)}) collective-permute-start(bf16[256,1024]{1,0:T(8,128)(2,1)} %slice.192), channel_id=1, source_target_pairs={{0,2},{1,3},{2,0},{3,1},{4,6},{5,7},{6,4},{7,5},{8,10},{9,11},{10,... | collective-permute-start | bytes 1572872 | tf_op jit(solution)/shard_map/ppermute | solution.py:236
  968.3 73.3 %copy-start.19 = (bf16[256,2048]{1,0:T(8,128)(2,1)S(1)}, bf16[256,2048]{1,0:T(8,128)(2,1)}, u32[]{:S(2)}) copy-start(bf16[256,2048]{1,0:T(8,128)(2,1)} %reduce-scatter.14.cloned.1.call-done) | copy-start | bytes 3145732
  972.4 114.2 %copy-start.20 = (bf16[256,2048]{1,0:T(8,128)(2,1)S(1)}, bf16[256,2048]{1,0:T(8,128)(2,1)}, u32[]{:S(2)}) copy-start(bf16[256,2048]{1,0:T(8,128)(2,1)} %reduce-scatter.12.cloned.1.call-done) | copy-start | bytes 3145732
  974.4 122.7 %collective-permute-start.17 = (bf16[256,1024]{1,0:T(8,128)(2,1)}, bf16[256,1024]{1,0:T(8,128)(2,1)}, u32[]{:S(2)}, u32[]{:S(2)}) collective-permute-start(bf16[256,1024]{1,0:T(8,128)(2,1)} %slice.190), channel_id=1, source_target_pairs={{0,2},{1,3},{2,0},{3,1},{4,6},{5,7},{6,4},{7,5},{8,10},{9,11},{10,... | collective-permute-start | bytes 1572872 | tf_op jit(solution)/shard_map/ppermute | solution.py:236
  1042.9 54.2 %copy-start.21 = (bf16[256,2048]{1,0:T(8,128)(2,1)S(1)}, bf16[256,2048]{1,0:T(8,128)(2,1)}, u32[]{:S(2)}) copy-start(bf16[256,2048]{1,0:T(8,128)(2,1)} %reduce-scatter.10.cloned.1.call-done) | copy-start | bytes 3145732
  (24 other events, 93.7 us)
Sparse Core Ops, SparseCore 0:
  12.7 74.7 all-gather.7
  89.3 72.6 all-gather.5
  164.5 56.2 all-gather.9
  222.5 54.2 all-gather.11
  278.5 55.8 all-gather.13
  552.4 71.4 reduce-scatter.13
  689.6 92.1 reduce-scatter.7
  785.3 71.4 reduce-scatter.11
  860.3 72.0 reduce-scatter.9
  935.7 92.0 reduce-scatter.5

commit v2 on v1

--- a/solution.py
+++ b/solution.py
@@ -41,6 +41,10 @@
 
 def dot_tn(left, right):
     return lax.dot_general(left, right, (((0,), (0,)), ((), ())), preferred_element_type=F32)
+
+
+def hold(value, *others):
+    return lax.optimization_barrier((value,) + others)[0]
 
 
 def turn(lead, trail, cosine, sinusoid):
@@ -116,10 +120,11 @@
 
 
 def retain_back_kernel(
-    decay_ref, keyr_ref, keyc_ref, cos_ref, sin_ref, qr_ref, kr_ref, vb_ref, g_ref, kept_ref, up_ref, gain_ref, bias_ref,
-    grad_ref, dgain_ref, dbias_ref,
-    dv_acc, dk_acc,
+    decay_ref, keyr_ref, keyc_ref, cos_ref, sin_ref, qr_ref, kr_ref, vb_ref, g_ref, kept_ref, gain_ref, bias_ref,
+    *rest,
 ):
+    *up_refs, grad_ref, dgain_ref, dbias_ref, dv_acc, dk_acc = rest
+    block = up_refs[0].shape[0]
     head = pl.program_id(0)
     heads = pl.num_programs(0)
     decay = decay_ref[head]
@@ -143,7 +148,7 @@
         unit = centred * inverse
         gate = g_ref[rows, :]
         open_gate = jax.nn.sigmoid(gate)
-        up = up_ref[rows, :]
+        up = up_refs[first // block][first % block : first % block + ROWS, :]
         grouped_grad = up * (gate * open_gate)
         gate_grad = up * (unit * gain + bias) * (open_gate * (1.0 + gate * (1.0 - open_gate)))
         grad_ref[rows, pl.ds(at_g, DV)] = gate_grad.astype(BF16)
@@ -175,8 +180,9 @@
     dbias_ref[...] = dbias
 
 
-def retain_back(decays, keyr, keyc, cosine, sinusoid, qr, kr, vb, pre, kept, up, gain, bias, place, heads):
+def retain_back(decays, keyr, keyc, cosine, sinusoid, qr, kr, vb, pre, kept, ups, gain, bias, place, heads):
     length = pre.shape[0]
+    block = ups[0].shape[0]
     whole = lambda shape: pl.BlockSpec(shape, lambda h: (0,) * len(shape))
     cols = lambda width, start: pl.BlockSpec((length, width), lambda h: (0, start + h))
     vec = pl.BlockSpec((1, DV), lambda h: (0, h))
@@ -187,9 +193,10 @@
             pl.BlockSpec(memory_space=pltpu.SMEM),
             whole((length, 1)), whole((1, length)),
             whole((length, DK // 2)), whole((length, DK // 2)),
-            cols(DK, 0), cols(DK, 0), cols(DV, 0), cols(DV, 2 * heads), cols(DV, 0), cols(DV, place * heads),
+            cols(DK, 0), cols(DK, 0), cols(DV, 0), cols(DV, 2 * heads), cols(DV, 0),
             vec, vec,
-        ],
+        ]
+        + [pl.BlockSpec((block, DV), lambda h: (0, place * heads + h))] * len(ups),
         out_specs=[whole((length, heads * 2 * (DK + DV))), vec, vec],
         out_shape=[
             jax.ShapeDtypeStruct((length, heads * 2 * (DK + DV)), BF16),
@@ -203,7 +210,7 @@
             transcendentals=heads * length * length,
         ),
         name="retain_back",
-    )(decays, keyr, keyc, cosine, sinusoid, qr, kr, vb, pre, kept, up, gain, bias)
+    )(decays, keyr, keyc, cosine, sinusoid, qr, kr, vb, pre, kept, gain, bias, *ups)
 
 
 def shards(
@@ -241,18 +248,16 @@
     def pick(array, shift):
         return lax.dynamic_index_in_dim(array, (mine + shift) % batches, 0, keepdims=False)
 
-    def own_rows(array):
-        return jnp.concatenate(
-            [pick(array, 0)[0]] + [across(pick(array, s)[0], s) for s in range(1, batches)], axis=0
-        )
-
     def gather_team(value):
         return [value] + [along_team(value, s) for s in range(1, teams)]
 
-    def scatter_team(part_of):
-        sent = [along_team(part_of(s).astype(BF16), teams - s) for s in range(1, teams)]
-        total = part_of(0)
-        for received in sent:
+    def send_parts(part_of):
+        return [along_team(part_of(s).astype(BF16), teams - s) for s in range(1, teams)]
+
+    def add_parts(total, sent, *fillers):
+        held = lax.optimization_barrier((total, *sent, *fillers))
+        total = held[0]
+        for received in held[1 : 1 + len(sent)]:
             total = total + received.astype(F32)
         return total
 
@@ -294,22 +299,18 @@
     group_gains = [v[None] for v in cut(group_gain_all, channels)]
     group_biases = [v[None] for v in cut(group_bias_all, channels)]
 
+    far = range(1, batches)
     mixer_shard = jnp.concatenate([w_query, w_key, w_value, w_gate], axis=1)
-    output_shard = w_output.T
-    inner_shard = w_inner
-    outer_shard = w_outer.T
-    token_rows = own_rows(tokens)
-    mixer_shards = [mixer_shard] + [across(mixer_shard, s) for s in range(1, batches)]
+    token_pieces = [pick(tokens, 0)[0]] + [across(pick(tokens, s)[0], s) for s in far]
+    mixer_shards = [mixer_shard] + [across(hold(mixer_shard, *token_pieces[1:]), s) for s in far]
     mixers = [lax.all_gather(s, "fsdp", axis=0, tiled=True) for s in mixer_shards]
-
-    def both(shard):
-        return jnp.concatenate([shard] + [across(shard, s) for s in range(1, batches)], axis=1)
-
-    output_full = lax.all_gather(both(output_shard), "fsdp", axis=0, tiled=True)
-    inner_full = lax.all_gather(both(inner_shard), "fsdp", axis=0, tiled=True)
-    outer_full = lax.all_gather(both(outer_shard), "fsdp", axis=0, tiled=True)
-    grad_rows = own_rows(cotangent)
-    grad_blocks = gather_team(grad_rows)
+    def both(shard, *after):
+        return jnp.concatenate([shard] + [across(hold(shard, *after), s) for s in far], axis=1)
+
+    def gather_rows(shard):
+        return lax.all_gather(shard, "fsdp", axis=0, tiled=True)
+
+    output_full = gather_rows(both(w_output.T, *mixer_shards[1:]))
 
     segments = pick(segment, 0)[0]
     length = segments.shape[0]
@@ -330,88 +331,144 @@
         for q in own_quarters
     ]
 
-    rows_in = token_rows.astype(F32)
-    normed_one, norm1_back = jax.vjp(layer_norm, rows_in, norm1_gain, norm1_bias)
-    normed_one_all = jnp.concatenate(gather_team(normed_one.astype(BF16)), axis=0)
+    normed_pieces = [
+        layer_norm(t.astype(F32), norm1_gain, norm1_bias).astype(BF16) for t in token_pieces
+    ]
+    gathered = [gather_team(p) for p in normed_pieces]
+    normed_one_all = jnp.concatenate(
+        [gathered[s][r] for r in range(teams) for s in range(batches)], axis=0
+    )
+    rows_in = jnp.concatenate(token_pieces, axis=0).astype(F32)
+    norm1_back = jax.vjp(layer_norm, rows_in, norm1_gain, norm1_bias)[1]
+    inner_both, outer_both = both(w_inner, *mixer_shards[1:]), both(w_outer.T, *mixer_shards[1:])
+    grad_pieces = [pick(cotangent, 0)[0]] + [
+        across(hold(pick(cotangent, s)[0], inner_both, outer_both), s) for s in far
+    ]
+    grads_gathered = [gather_team(p) for p in grad_pieces]
+    grad_blocks = [
+        jnp.concatenate([grads_gathered[s][r] for s in range(batches)], axis=0) for r in range(teams)
+    ]
+    grad_rows = grad_blocks[0]
     gated = jnp.zeros((length, batches * channels), BF16)
     saved = []
     for s in range(batches):
         pre = dot_nn(normed_one_all, mixers[s])
+        if s == 0:
+            inner_full = gather_rows(hold(inner_both, pre))
         gated, kept, qr, kr, vb = retain(
             decays[s], keyr, keyc, cosine, sinusoid, pre, group_gains[s], group_biases[s], gated, s, heads
         )
         saved.append((pre, kept, qr, kr, vb))
+    outer_full = gather_rows(hold(outer_both, pre))
     block = batches * piece
 
     def rows_of(array, r):
         return array[r * block : (r + 1) * block]
 
-    hidden = rows_in + scatter_team(lambda r: dot_nt(rows_of(gated, r), output_full))
+    def output_part(r):
+        return dot_nt(rows_of(gated, r), output_full)
+
+    sent = send_parts(output_part)
+    hidden = rows_in + add_parts(output_part(0), sent)
     normed_two, norm2_back = jax.vjp(layer_norm, hidden, norm2_gain, norm2_bias)
-    normed_two_blocks = gather_team(normed_two.astype(BF16))
-    active_blocks, slope_blocks = [], []
-    for normed in normed_two_blocks:
+
+    def activate(normed):
         inner = dot_nn(normed, inner_full) + inner_bias
         below = 0.5 * (1.0 + lax.erf(inner * (0.5**0.5)))
-        active_blocks.append((inner * below).astype(BF16))
         bell = jnp.exp(-0.5 * inner * inner) * ((2.0 * jnp.pi) ** -0.5)
-        slope_blocks.append((below + inner * bell).astype(BF16))
-
-    inner_grad_blocks = [
-        (slope.astype(F32) * dot_nn(grad, outer_full)).astype(BF16)
-        for slope, grad in zip(slope_blocks, grad_blocks)
-    ]
-    normed_two_grad = scatter_team(lambda r: dot_nt(inner_grad_blocks[r], inner_full))
+        return (inner * below).astype(BF16), (below + inner * bell).astype(BF16)
+
+    normed_two_blocks = gather_team(normed_two.astype(BF16))
+    first = activate(normed_two_blocks[0])
+    normed_two_blocks[1:] = [hold(n, *first) for n in normed_two_blocks[1:]]
+    active_blocks, slope_blocks = zip(first, *[activate(n) for n in normed_two_blocks[1:]])
+
+    def inner_grad_of(r):
+        return (slope_blocks[r].astype(F32) * dot_nn(grad_blocks[r], outer_full)).astype(BF16)
+
+    inner_grad_blocks = [None] * teams
+    sent = []
+    for r in range(1, teams):
+        inner_grad_blocks[r] = inner_grad_of(r)
+        sent.append(along_team(dot_nt(inner_grad_blocks[r], inner_full).astype(BF16), teams - r))
+    inner_grad_blocks[0] = inner_grad_of(0)
+
+    def reduce_columns(whole):
+        return lax.psum_scatter(whole, "fsdp", scatter_dimension=0, tiled=True)
+
+    def trade(parts):
+        return [parts[0]] + [across(parts[s], batches - s) for s in far]
+
+    def settle(parts):
+        total = parts[0].astype(F32)
+        for part in parts[1:]:
+            total = total + part.astype(F32)
+        return total
+
+    def settle_both(whole):
+        size = whole.shape[1] // batches
+        return settle(trade([whole[:, s * size : (s + 1) * size] for s in range(batches)]))
+
+    active_all = jnp.concatenate(active_blocks, axis=0)
+    grad_all = jnp.concatenate(grad_blocks, axis=0)
+    outer_sum = dot_tn(grad_all, active_all).astype(BF16)
+    normed_two_grad = add_parts(dot_nt(inner_grad_blocks[0], inner_full), sent, outer_sum)
     hidden_part, norm2_gain_sum, norm2_bias_sum = norm2_back(normed_two_grad)
     hidden_grad = grad_rows.astype(F32) + hidden_part
-    hidden_low_all = jnp.concatenate(gather_team(hidden_grad.astype(BF16)), axis=0)
-
-    result = hidden + scatter_team(lambda r: dot_nt(active_blocks[r], outer_full)) + outer_bias
-    out = give_back(result.astype(BF16))
-
-    def reduce_columns(whole):
-        return lax.psum_scatter(whole.astype(BF16), "fsdp", scatter_dimension=0, tiled=True)
-
-    def settle(parts):
-        total = parts[0].astype(F32)
-        for s in range(1, batches):
-            total = total + across(parts[s], batches - s).astype(F32)
-        return total
-
-    def settle_both(whole):
-        size = whole.shape[1] // batches
-        return settle([whole[:, s * size : (s + 1) * size] for s in range(batches)])
-
-    active_all = jnp.concatenate(active_blocks, axis=0)
-    grad_all = jnp.concatenate(grad_blocks, axis=0)
+    hidden_low_blocks = gather_team(hidden_grad.astype(BF16))
+
     inner_grad_all = jnp.concatenate(inner_grad_blocks, axis=0)
     normed_two_all = jnp.concatenate(normed_two_blocks, axis=0)
-    grad_outer = settle_both(reduce_columns(dot_tn(grad_all, active_all))).T
-    grad_inner = settle_both(reduce_columns(dot_tn(normed_two_all, inner_grad_all)))
+    inner_sum = dot_tn(normed_two_all, inner_grad_all).astype(BF16)
     inner_bias_sum = jnp.sum(inner_grad_all.astype(F32), axis=0)
     outer_bias_sum = jnp.sum(grad_rows.astype(F32), axis=0)
-
-    gated_grad = dot_nn(hidden_low_all, output_full)
-    grads, gain_sums, bias_sums, mixer_sums = [], [], [], []
+    result_parts = [dot_nt(active_blocks[r], outer_full).astype(BF16) for r in range(1, teams)]
+    result_own = dot_nt(active_blocks[0], outer_full)
+    ups = [dot_nn(hidden_low_blocks[0], output_full)]
+    hidden_low_blocks[1:] = [
+        hold(h, inner_sum, ups[0], *result_parts) for h in hidden_low_blocks[1:]
+    ]
+    grad_outer = settle_both(reduce_columns(outer_sum)).T
+    inner_reduced = reduce_columns(inner_sum)
+    grad_inner = settle_both(inner_reduced)
+
+    sent = [
+        along_team(hold(p, *hidden_low_blocks[1:]), teams - 1 - i) for i, p in enumerate(result_parts)
+    ]
+    result = hidden + add_parts(result_own, sent) + outer_bias
+    out = give_back(result.astype(BF16))
+
+    ups += [dot_nn(h, output_full) for h in hidden_low_blocks[1:]]
+    hidden_low_all = jnp.concatenate(hidden_low_blocks, axis=0)
+    grads, gain_sums, bias_sums = [], [], []
+    late, ready = (), ()
     for s in reversed(range(batches)):
         pre, kept, qr, kr, vb = saved[s]
         grad, gain_sum, bias_sum = retain_back(
-            decays[s], keyr, keyc, cosine, sinusoid, qr, kr, vb, pre, kept, gated_grad,
+            decays[s], keyr, keyc, cosine, sinusoid, hold(qr, *late, *ready), kr, vb, pre, kept, ups,
             group_gains[s], group_biases[s], s, heads,
         )
         grads.insert(0, grad)
         gain_sums.insert(0, gain_sum[0])
         bias_sums.insert(0, bias_sum[0])
-        mixer_sums.insert(0, reduce_columns(dot_tn(normed_one_all, grad)))
-    grad_output = settle_both(reduce_columns(dot_tn(hidden_low_all, gated))).T
+        if s:
+            late = late + (dot_tn(normed_one_all, grad).astype(BF16),)
+            ready = (result, grad_outer)
 
     def normed_one_part(r):
         total = dot_nt(rows_of(grads[0], r), mixers[0])
-        for s in range(1, batches):
+        for s in far:
             total = total + dot_nt(rows_of(grads[s], r), mixers[s])
         return total
 
-    normed_one_grad = scatter_team(normed_one_part)
+    sent = send_parts(normed_one_part)
+    output_sum = dot_tn(hidden_low_all, gated).astype(BF16)
+    far_sums = [reduce_columns(hold(m, inner_reduced)) for m in late[::-1]]
+    own_sum = dot_tn(hold(normed_one_all, output_sum, grad_inner, *far_sums), grads[0]).astype(BF16)
+    far_traded = trade([grads[0]] + far_sums)[1:]
+    grad_output = settle_both(reduce_columns(output_sum)).T
+    mixer_sums = [reduce_columns(own_sum)] + far_traded
+    normed_one_grad = add_parts(normed_one_part(0), sent, output_sum, own_sum, *far_traded)
     input_part, norm1_gain_sum, norm1_bias_sum = norm1_back(normed_one_grad)
     input_grad = give_back(hidden_grad + input_part)
     grad_mixer = settle(mixer_sums)

time: 1120 us -> 1050 us (0.938)
  waiting for transfers between devices: 626 us -> 556 us
  other arithmetic: 45.3 us -> 62.6 us
  matrix products: 285 us -> 273 us
    all_to_all x2, waiting for transfers between devices: 92.8 us -> 43.4 us  [exchange(): lax.all_to_all(padded, ('fsdp', 'tp'), 0, 0, tiled=True)]
    ppermute x8 -> x10, waiting for transfers between devices: 298 us -> 274 us  [along_team(): return lax.ppermute(value, 'tp', route)]
    dot_general x7 -> x8, matrix products: 90.8 us -> 85.4 us  [dot_nn(): lax.dot_general(left, right, (((1,), (0,)), ((), ())), preferred_element_...]
  transfers between devices with their start and end apart: 32 -> 34, of which waited for: 16 -> 19; matrix products, arithmetic and copies ran while one was open for 30% -> 32% of each run, Pallas kernels for 6% -> 7%
where the time goes in v2:
time: 1050 us
  waiting for transfers between devices  556 us (53%)
  matrix products  273 us (26%)
  Pallas kernels  69.9 us (7%)
  other arithmetic  62.6 us (6%)
  local copies, waits for them, and re-layouts  38.7 us (4%)
  starting transfers between devices  30.5 us (3%)
  between operations  15.8 us (2%)
    ppermute x10, waiting for transfers between devices, along_team(): return lax.ppermute(value, 'tp', route)  274 us
    ppermute x12, waiting for transfers between devices, across(): return lax.ppermute(value, 'tp', route)  238 us
    dot_general x10, matrix products, dot_nt(): lax.dot_general(left, right, (((1,), (1,)), ((), ())), preferred_element_...  106 us
    dot_general x8, matrix products, dot_nn(): lax.dot_general(left, right, (((1,), (0,)), ((), ())), preferred_element_...  85.4 us
    dot_general x5, matrix products, dot_tn(): lax.dot_general(left, right, (((0,), (0,)), ((), ())), preferred_element_...  81.2 us
    pallas_call x2, Pallas kernels, retain_back(): pl.pallas_call(retain_back_kernel, grid=(heads,), in_specs=[pl.BlockSpec(...  44.3 us
    all_to_all x2, waiting for transfers between devices, exchange(): lax.all_to_all(padded, ('fsdp', 'tp'), 0, 0, tiled=True)  43.4 us
    pallas_call x2, Pallas kernels, retain(): pl.pallas_call(retain_kernel, grid=(heads,), in_specs=[pl.BlockSpec(memor...  25.6 us
  transfers between devices with their start and end apart: 34, of which 19 were waited for; matrix products, arithmetic and copies ran while one was open for 32% of the time, Pallas kernels for 7%

profile of v2, /device:TPU:0, one launch (start us, length us, event | category | flops | bytes accessed | tf_op | source)
XLA Modules:
  0.0 1046.6 jit_solution(5044730831373014983)
XLA Ops:
  14.0 4.1 collective-permute-start
  18.1 45.6 %collective-permute-done = bf16[256,2048]{1,0:T(8,128)(2,1)S(1)} collective-permute-done((bf16[256,2048]{1,0:T(8,128)(2,1)S(1)}, bf16[256,2048]{1,0:T(8,128)(2,1)S(1)}, u32[]{:S(2)}, u32[]{:S(2)}) %collective-permute-start) | collective-permute-done | bytes 1048608 | tf_op jit(solution)/shard_map/ppermute | solution.py:243
  63.7 70.4 %collective-permute-done.3 = bf16[256,3072]{1,0:T(8,128)(2,1)S(1)} collective-permute-done((bf16[256,3072]{1,0:T(8,128)(2,1)}, bf16[256,3072]{1,0:T(8,128)(2,1)S(1)}, u32[]{:S(2)}, u32[]{:S(2)}) %collective-permute-start.3) | collective-permute-done | bytes 1572896 | tf_op jit(solution)/shard_map/ppermute | solution.py:243
  135.4 24.4 %collective-permute-done.4 = bf16[256,1024]{0,1:T(8,128)(2,1)S(1)} collective-permute-done((bf16[256,1024]{0,1:T(8,128)(2,1)S(1)}, bf16[256,1024]{0,1:T(8,128)(2,1)S(1)}, u32[]{:S(2)}, u32[]{:S(2)}) %collective-permute-start.4) | collective-permute-done | bytes 524320 | tf_op jit(solution)/shard_map/ppermute | solution.py:243
  161.7 3.0 all-to-all-start
  166.6 6.5 all-to-all-done
  180.5 52.7 %collective-permute-done.6 = bf16[256,1024]{1,0:T(8,128)(2,1)S(1)} collective-permute-done((bf16[256,1024]{1,0:T(8,128)(2,1)}, bf16[256,1024]{1,0:T(8,128)(2,1)S(1)}, u32[]{:S(2)}, u32[]{:S(2)}) %collective-permute-start.6) | collective-permute-done | bytes 524320 | tf_op jit(solution)/shard_map/ppermute | solution.py:243
  234.6 19.6 %fusion.78.q_ref.k_ref.v_ref.g_ref = f32[1024,3072]{1,0:T(8,128)} fusion(bf16[2048,3072]{1,0:T(8,128)(2,1)} %all-gather.8.cloned.1.call-done, bf16[256,2048]{1,0:T(8,128)(2,1)} %collective-permute-done.2, bf16[256,2048]{1,0:T(8,128)(2,1)} %collective-permute-done.1, bf16[256,2048]{1,0:T(8,128)(2,1)} %get-tuple-element.171, ...), kind=kOutput, calls=%fused_computation.173 | convolution fusion | flops 12901679104 | bytes 29360128 | tf_op jit(solution)/shard_map/dot_general | solution.py:35
  254.3 3.0 collective-permute-start.7
  257.2 22.6 %collective-permute-done.7 = bf16[256,1024]{0,1:T(8,128)(2,1)S(1)} collective-permute-done((bf16[256,1024]{0,1:T(8,128)(2,1)}, bf16[256,1024]{0,1:T(8,128)(2,1)S(1)}, u32[]{:S(2)}, u32[]{:S(2)}) %collective-permute-start.7) | collective-permute-done | bytes 524320 | tf_op jit(solution)/shard_map/ppermute | solution.py:243
  279.8 2.1 pad_maximum_fusion.6
  281.9 18.7 %fusion.79.q_ref.k_ref.v_ref.g_ref = f32[1024,3072]{1,0:T(8,128)} fusion(bf16[2048,3072]{1,0:T(8,128)(2,1)} %all-gather.6.cloned.1.call-done, bf16[256,2048]{1,0:T(8,128)(2,1)} %collective-permute-done.2, bf16[256,2048]{1,0:T(8,128)(2,1)} %collective-permute-done.1, bf16[256,2048]{1,0:T(8,128)(2,1)} %get-tuple-element.171, ...), kind=kOutput, calls=%fused_computation.174 | convolution fusion | flops 12901679104 | bytes 29360128 | tf_op jit(solution)/shard_map/dot_general | solution.py:35
  304.0 3.0 multiply_sine_fusion
  308.3 2.5 broadcast_in_dim.66.held_ref
  310.8 12.8 %retain.2 = (bf16[1024,2048]{1,0:T(8,128)(2,1)}, f32[1024,1024]{1,0:T(8,128)}, bf16[1024,512]{1,0:T(8,128)(2,1)}, bf16[1024,512]{1,0:T(8,128)(2,1)}, bf16[1024,1024]{1,0:T(8,128)(2,1)}) custom-call(f32[2]{0:T(128)} %negate_log-plus-one_fusion.decay_ref, f32[1024,1]{1,0:T(8,128)} %copy.42.keyr_ref, ...), custom_call_target="tpu_custom_call", output_to_operand_aliasing={{0}: (11, {})} | custom-call | flops 3221225472 | bytes 23068672 | tf_op jit(solution)/shard_map/retain/pallas_call | solution.py:93
  323.7 12.7 %retain.3 = (bf16[1024,2048]{1,0:T(8,128)(2,1)}, f32[1024,1024]{1,0:T(8,128)}, bf16[1024,512]{1,0:T(8,128)(2,1)}, bf16[1024,512]{1,0:T(8,128)(2,1)}, bf16[1024,1024]{1,0:T(8,128)(2,1)}) custom-call(f32[2]{0:T(128)} %negate_log-plus-one_fusion.1.decay_ref, f32[1024,1]{1,0:T(8,128)} %copy.42.keyr_ref, ...), custom_call_target="tpu_custom_call", output_to_operand_aliasing={{0}: (11, {})} | custom-call | flops 3221225472 | bytes 23068672 | tf_op jit(solution)/shard_map/retain/pallas_call | solution.py:93
  336.5 9.9 convolution_convert_fusion.7
  349.8 8.2 fusion.66
  358.1 57.8 %collective-permute-done.5 = bf16[512,2048]{1,0:T(8,128)(2,1)} collective-permute-done((bf16[512,2048]{1,0:T(8,128)(2,1)}, bf16[512,2048]{1,0:T(8,128)(2,1)}, u32[]{:S(2)}, u32[]{:S(2)}) %collective-permute-start.5) | collective-permute-done | bytes 2097184 | tf_op jit(solution)/shard_map/ppermute | solution.py:237
  415.8 3.9 fusion.82
  423.8 9.8 fusion.12
  433.6 36.7 %collective-permute-done.8 = bf16[512,2048]{1,0:T(8,128)(2,1)} collective-permute-done((bf16[512,2048]{1,0:T(8,128)(2,1)S(1)}, bf16[512,2048]{1,0:T(8,128)(2,1)}, u32[]{:S(2)}, u32[]{:S(2)}) %collective-permute-start.8) | collective-permute-done | bytes 2097184 | tf_op jit(solution)/shard_map/ppermute | solution.py:237
  470.3 8.4 multiply_convert_fusion.2
  478.8 9.0 multiply_convert_fusion.1
  487.8 5.0 collective-permute-done.10
  492.8 19.7 %collective-permute-done.11 = bf16[256,2048]{1,0:T(8,128)(2,1)} collective-permute-done((bf16[256,2048]{1,0:T(8,128)(2,1)}, bf16[256,2048]{1,0:T(8,128)(2,1)}, u32[]{:S(2)}, u32[]{:S(2)}) %collective-permute-start.11) | collective-permute-done | bytes 1048608 | tf_op jit(solution)/shard_map/ppermute | solution.py:237
  512.5 7.5 multiply_convert_fusion
  521.4 12.9 %convolution_convert_fusion.3 = bf16[2048,2048]{1,0:T(8,128)(2,1)} fusion(bf16[512,2048]{1,0:T(8,128)(2,1)} %collective-permute-done.8, bf16[512,2048]{1,0:T(8,128)(2,1)S(1)} %copy-done.23, bf16[512,2048]{1,0:T(8,128)(2,1)S(1)} %multiply_convert_fusion, bf16[512,2048]{1,0:T(8,128)(2,1)S(1)} %multiply_convert_fusion.1), kind=kOutput, calls=%fused_computation.4 | convolution fusion | flops 8610906112 | bytes 16777216 | tf_op jit(solution)/shard_map/dot_general | solution.py:43
  534.4 14.8 %convolution_convert_fusion.4 = bf16[2048,2048]{1,0:T(8,128)(2,1)} fusion(bf16[256,2048]{1,0:T(8,128)(2,1)} %collective-permute-done.11, bf16[256,2048]{1,0:T(8,128)(2,1)} %collective-permute-done.10, bf16[256,2048]{1,0:T(8,128)(2,1)} %collective-permute-done.9, bf16[256,2048]{1,0:T(8,128)(2,1)S(1)} %get-tuple-element.154, ...), kind=kOutput, calls=%fused_computation.5 | convolution fusion | flops 8619294720 | bytes 16777216 | tf_op jit(solution)/shard_map/dot_general | solution.py:43
  549.2 8.5 convolution_convert_fusion.5
  557.9 7.6 fusion.94
  565.5 37.3 %collective-permute-done.12 = bf16[512,2048]{1,0:T(8,128)(2,1)S(1)} collective-permute-done((bf16[512,2048]{1,0:T(8,128)(2,1)S(1)}, bf16[512,2048]{1,0:T(8,128)(2,1)S(1)}, u32[]{:S(2)}, u32[]{:S(2)}) %collective-permute-start.12) | collective-permute-done | bytes 2097184 | tf_op jit(solution)/shard_map/ppermute | solution.py:237
  602.8 2.1 multiply_reduce_fusion
  606.8 2.8 fusion.47
  610.6 5.9 convolution_convert_fusion.6
  616.5 6.2 fusion.95.rest_0_
  622.7 31.4 %collective-permute-done.13 = bf16[512,2048]{1,0:T(8,128)(2,1)S(1)} collective-permute-done((bf16[512,2048]{1,0:T(8,128)(2,1)S(1)}, bf16[512,2048]{1,0:T(8,128)(2,1)S(1)}, u32[]{:S(2)}, u32[]{:S(2)}) %collective-permute-start.13) | collective-permute-done | bytes 2097184 | tf_op jit(solution)/shard_map/ppermute | solution.py:237
  654.1 6.2 fusion.96.rest_1_
  660.2 22.2 %retain_back.2 = (bf16[1024,3072]{1,0:T(8,128)(2,1)}, f32[1,1024]{1,0:T(1,128)}, f32[1,1024]{1,0:T(1,128)}) custom-call(f32[2]{0:T(128)} %negate_log-plus-one_fusion.1.decay_ref, f32[1024,1]{1,0:T(8,128)} %copy.42.keyr_ref, f32[1,1024]{1,0:T(1,128)} %bitcast.110, f32[1024,128]{1,0:T(8,128)} %get-tuple-element.173.cos_ref, ...), custom_call_target="tpu_custom_call" | custom-call | flops 7516192768 | bytes 23068672 | tf_op jit(solution)/shard_map/retain_back/pallas_call | solution.py:189
  682.4 19.3 %convolution_convert_fusion.1 = bf16[2048,3072]{1,0:T(8,128)(2,1)} fusion(bf16[1024,3072]{1,0:T(8,128)(2,1)} %get-tuple-element.77, bf16[256,2048]{1,0:T(8,128)(2,1)} %collective-permute-done.2, bf16[256,2048]{1,0:T(8,128)(2,1)} %collective-permute-done.1, bf16[256,2048]{1,0:T(8,128)(2,1)} %get-tuple-element.171, bf16[256,2048]{1,0:T(8,128)(2,1)S(1)} %copy-done.15), kind=kOutput, calls=%fused_computation.1 | convolution fusion | flops 12907970560 | bytes 23068672 | tf_op jit(solution)/shard_map/dot_general | solution.py:43
  703.3 14.4 %convolution_convert_fusion.2 = bf16[2048,2048]{1,0:T(8,128)(2,1)} fusion(bf16[1024,2048]{1,0:T(8,128)(2,1)} %get-tuple-element.56, bf16[512,2048]{1,0:T(8,128)(2,1)} %copy-done.53, bf16[512,2048]{1,0:T(8,128)(2,1)S(1)} %copy-done.18), kind=kOutput, calls=%fused_computation.3 | convolution fusion | flops 8602517504 | bytes 16777216 | tf_op jit(solution)/shard_map/dot_general | solution.py:43
  719.6 4.4 pad_maximum_fusion
  724.0 9.4 fusion.93
  733.4 28.9 %collective-permute-done.14 = bf16[512,2048]{1,0:T(8,128)(2,1)S(1)} collective-permute-done((bf16[512,2048]{1,0:T(8,128)(2,1)}, bf16[512,2048]{1,0:T(8,128)(2,1)S(1)}, u32[]{:S(2)}, u32[]{:S(2)}) %collective-permute-start.14) | collective-permute-done | bytes 2097184 | tf_op jit(solution)/shard_map/ppermute | solution.py:237
  763.9 5.5 add_add_fusion.3
  769.4 15.1 %collective-permute-done.16 = bf16[256,1024]{1,0:T(8,128)(2,1)S(1)} collective-permute-done((bf16[256,1024]{1,0:T(8,128)(2,1)S(1)}, bf16[256,1024]{1,0:T(8,128)(2,1)S(1)}, u32[]{:S(2)}, u32[]{:S(2)}) %collective-permute-start.16) | collective-permute-done | bytes 524320 | tf_op jit(solution)/shard_map/ppermute | solution.py:243
  785.6 22.2 %retain_back.3 = (bf16[1024,3072]{1,0:T(8,128)(2,1)}, f32[1,1024]{1,0:T(1,128)}, f32[1,1024]{1,0:T(1,128)}) custom-call(f32[2]{0:T(128)} %negate_log-plus-one_fusion.decay_ref, f32[1024,1]{1,0:T(8,128)} %copy.42.keyr_ref, f32[1,1024]{1,0:T(1,128)} %bitcast.111, f32[1024,128]{1,0:T(8,128)} %get-tuple-element.173.cos_ref, ...), custom_call_target="tpu_custom_call" | custom-call | flops 7516192768 | bytes 23068672 | tf_op jit(solution)/shard_map/retain_back/pallas_call | solution.py:189
  809.1 2.6 convert_add_fusion.5
  811.7 19.8 %convolution_convert_fusion = bf16[2048,3072]{1,0:T(8,128)(2,1)} fusion(bf16[1024,2048]{1,0:T(8,128)(2,1)} %pad_maximum_fusion, bf16[1024,3072]{1,0:T(8,128)(2,1)} %get-tuple-element.82), kind=kOutput, calls=%fused_computation | convolution fusion | flops 12891193344 | bytes 23068672 | tf_op jit(solution)/shard_map/dot_general | solution.py:43
  832.1 3.0 convert_reduce_fusion
  838.1 12.0 %fusion.36 = f32[512,2048]{1,0:T(8,128)} fusion(bf16[2048,3072]{1,0:T(8,128)(2,1)} %all-gather.8.cloned.1.call-done, bf16[1024,3072]{1,0:T(8,128)(2,1)} %get-tuple-element.82), kind=kOutput, calls=%fused_computation.70 | convolution fusion | flops 6442450944 | bytes 19922944 | tf_op jit(solution)/shard_map/dot_general | solution.py:39
  850.1 14.5 %add_convert_fusion = bf16[512,2048]{1,0:T(8,128)(2,1)} fusion(f32[512,2048]{1,0:T(8,128)} %fusion.36, bf16[2048,3072]{1,0:T(8,128)(2,1)} %all-gather.6.cloned.1.call-done, bf16[1024,3072]{1,0:T(8,128)(2,1)} %get-tuple-element.77), kind=kOutput, calls=%fused_computation.55 | convolution fusion | flops 6444548096 | bytes 22020096 | tf_op jit(solution)/shard_map/dot_general | solution.py:39
  866.2 12.0 %fusion.40 = f32[512,2048]{1,0:T(8,128)} fusion(bf16[2048,3072]{1,0:T(8,128)(2,1)} %all-gather.8.cloned.1.call-done, bf16[1024,3072]{1,0:T(8,128)(2,1)} %get-tuple-element.82), kind=kOutput, calls=%fused_computation.74 | convolution fusion | flops 6442450944 | bytes 19922944 | tf_op jit(solution)/shard_map/dot_general | solution.py:39
  878.9 18.2 %fusion.42 = f32[512,2048]{1,0:T(8,128)} fusion(f32[512,2048]{1,0:T(8,128)} %fusion.40, bf16[2048,3072]{1,0:T(8,128)(2,1)} %all-gather.6.cloned.1.call-done, bf16[1024,3072]{1,0:T(8,128)(2,1)} %get-tuple-element.77), kind=kOutput, calls=%fused_computation.76 | convolution fusion | flops 6443499520 | bytes 24117248 | tf_op jit(solution)/shard_map/dot_general | solution.py:39
  900.9 57.0 %collective-permute-done.17 = bf16[512,2048]{1,0:T(8,128)(2,1)} collective-permute-done((bf16[512,2048]{1,0:T(8,128)(2,1)}, bf16[512,2048]{1,0:T(8,128)(2,1)}, u32[]{:S(2)}, u32[]{:S(2)}) %collective-permute-start.17) | collective-permute-done | bytes 2097184 | tf_op jit(solution)/shard_map/ppermute | solution.py:237
  957.9 6.3 collective-permute-done.19
  964.3 4.3 fusion.7
  968.7 4.1 fusion.80
  972.8 2.7 convert_reduce_fusion.2
  984.2 4.7 all-to-all-start.1
  991.7 36.8 %all-to-all-done.1 = f32[32,6,128]{2,1,0:T(8,128)S(1)} async-done(((f32[32,6,128]{2,1,0:T(8,128)}), f32[32,6,128]{2,1,0:T(8,128)S(1)}, u32[]{:S(2)}, u32[]{:S(2)}) %all-to-all-start.1) | async-done | bytes 98336 | tf_op jit(solution)/shard_map/all_to_all | solution.py:284
  1029.7 2.4 fusion.60
  1032.2 2.3 maximum_bitcast_fusion
  1034.5 2.4 convert_add_fusion.4
  (274 shorter events, 68.8 us)
Async XLA Ops:
  7.2 128.1 %copy-start.28 = (bf16[1024,256]{1,0:T(8,128)(2,1)S(1)}, bf16[1024,256]{1,0:T(8,128)(2,1)}, u32[]{:S(2)}) copy-start(bf16[1024,256]{1,0:T(8,128)(2,1)} %param.26) | copy-start | bytes 1572868
  7.2 227.4 %all-gather.8.cloned.1.call-start = ((), (), s32[]{:S(2)}) async-start(), calls=%async_computation.8 | async-start | bytes 14155776 | tf_op jit(solution)/shard_map/all_gather | solution.py:306
  11.4 149.4 %copy-start.43 = (f32[64]{0:T(128)S(1)}, f32[64]{0:T(128)}, u32[]{:S(2)}) copy-start(f32[64]{0:T(128)} %param.20) | copy-start | bytes 772
  11.4 149.4 %copy-start.44 = (f32[64]{0:T(128)S(1)}, f32[64]{0:T(128)}, u32[]{:S(2)}) copy-start(f32[64]{0:T(128)} %param.21) | copy-start | bytes 772
  11.5 149.4 %copy-start.45 = (f32[64]{0:T(128)S(1)}, f32[64]{0:T(128)}, u32[]{:S(2)}) copy-start(f32[64]{0:T(128)} %param.29) | copy-start | bytes 772
  11.5 149.4 %copy-start.46 = (f32[64]{0:T(128)S(1)}, f32[64]{0:T(128)}, u32[]{:S(2)}) copy-start(f32[64]{0:T(128)} %param.30) | copy-start | bytes 772
  11.5 149.4 %copy-start.47 = (f32[64]{0:T(128)S(1)}, f32[64]{0:T(128)}, u32[]{:S(2)}) copy-start(f32[64]{0:T(128)} %param.34) | copy-start | bytes 772
  11.5 149.4 %copy-start.48 = (f32[128]{0:T(128)S(1)}, f32[128]{0:T(128)}, u32[]{:S(2)}) copy-start(f32[128]{0:T(128)} %param.32) | copy-start | bytes 1540
  11.5 149.4 %copy-start.49 = (f32[128]{0:T(128)S(1)}, f32[128]{0:T(128)}, u32[]{:S(2)}) copy-start(f32[128]{0:T(128)} %param.27) | copy-start | bytes 1540
  11.5 149.4 %copy-start.50 = (f32[128]{0:T(128)S(1)}, f32[128]{0:T(128)}, u32[]{:S(2)}) copy-start(f32[128]{0:T(128)} %param.28) | copy-start | bytes 1540
  12.6 269.3 %all-gather.6.cloned.1.call-start = ((), (), s32[]{:S(2)}) async-start(), calls=%async_computation.7 | async-start | bytes 14155776 | tf_op jit(solution)/shard_map/all_gather | solution.py:306
  14.0 49.8 %collective-permute-start = (bf16[256,2048]{1,0:T(8,128)(2,1)S(1)}, bf16[256,2048]{1,0:T(8,128)(2,1)S(1)}, u32[]{:S(2)}, u32[]{:S(2)}) collective-permute-start(bf16[256,2048]{1,0:T(8,128)(2,1)S(1)} %dynamic-slice_bitcast_fusion.2), channel_id=1, source_target_pairs={{0,2},{1,3},{2,0},{3,1},{4,6},{5,7},{6,4},{7,5},{8,10},{9,11},{10,... | collective-permute-start | bytes 3145736 | tf_op jit(solution)/shard_map/ppermute | solution.py:243
  63.7 352.1 %copy-start.2 = (bf16[256,2048]{1,0:T(8,128)(2,1)}, bf16[256,2048]{1,0:T(8,128)(2,1)S(1)}, u32[]{:S(2)}) copy-start(bf16[256,2048]{1,0:T(8,128)(2,1)S(1)} %collective-permute-done) | copy-start | bytes 3145732
  63.7 70.4 %collective-permute-start.3 = (bf16[256,3072]{1,0:T(8,128)(2,1)}, bf16[256,3072]{1,0:T(8,128)(2,1)S(1)}, u32[]{:S(2)}, u32[]{:S(2)}) collective-permute-start(bf16[256,3072]{1,0:T(8,128)(2,1)} %copy-done.16), channel_id=1, source_target_pairs={{0,2},{1,3},{2,0},{3,1},{4,6},{5,7},{6,4},{7,5},{8,10},{9,11},{10,... | collective-permute-start | bytes 4718600 | tf_op jit(solution)/shard_map/ppermute | solution.py:243
  135.3 201.2 %all-gather.10.cloned.1.call-start = ((), (), s32[]{:S(2)}) async-start(), calls=%async_computation.9 | async-start | bytes 9437184 | tf_op jit(solution)/shard_map/all_gather | solution.py:311
  135.3 24.4 %collective-permute-start.4 = (bf16[256,1024]{0,1:T(8,128)(2,1)S(1)}, bf16[256,1024]{0,1:T(8,128)(2,1)S(1)}, u32[]{:S(2)}, u32[]{:S(2)}) collective-permute-start(bf16[256,1024]{0,1:T(8,128)(2,1)S(1)} %bitcast.103), channel_id=1, source_target_pairs={{0,2},{1,3},{2,0},{3,1},{4,6},{5,7},{6,4},{7,5},{8,10},{9,11},{10,... | collective-permute-start | bytes 1572872 | tf_op jit(solution)/shard_map/ppermute | solution.py:243
  161.7 11.5 %all-to-all-start = ((f32[32,6,128]{2,1,0:T(8,128)}), f32[32,6,128]{2,1,0:T(8,128)S(1)}, u32[]{:S(2)}, u32[]{:S(2)}) async-start(f32[32,6,128]{2,1,0:T(8,128)} %pad.13), calls=%async_computation | async-start | bytes 262144 | tf_op jit(solution)/shard_map/all_to_all | solution.py:284
  164.7 259.1 %all-gather.12.cloned.1.call-start = ((), (), s32[]{:S(2)}) async-start(), calls=%async_computation.10 | async-start | bytes 9437184 | tf_op jit(solution)/shard_map/all_gather | solution.py:311
  166.2 249.6 %copy-start.4 = (bf16[256,2048]{1,0:T(8,128)(2,1)}, bf16[256,2048]{1,0:T(8,128)(2,1)S(1)}, u32[]{:S(2)}) copy-start(bf16[256,2048]{1,0:T(8,128)(2,1)S(1)} %get-tuple-element.138) | copy-start | bytes 3145732
  173.9 60.2 %copy-start.30 = (f32[2048]{0:T(1024)}, f32[2048]{0:T(1024)S(1)}, u32[]{:S(2)}) copy-start(f32[2048]{0:T(1024)S(1)} %mul.274) | copy-start | bytes 24580
  176.3 105.6 %copy-start.14 = (bf16[256,2048]{1,0:T(8,128)(2,1)}, bf16[256,2048]{1,0:T(8,128)(2,1)S(1)}, u32[]{:S(2)}) copy-start(bf16[256,2048]{1,0:T(8,128)(2,1)S(1)} %get-tuple-element.170) | copy-start | bytes 3145732
  176.3 57.8 %collective-permute-start.2 = (bf16[256,2048]{1,0:T(8,128)(2,1)}, bf16[256,2048]{1,0:T(8,128)(2,1)}, u32[]{:S(2)}, u32[]{:S(2)}) collective-permute-start(bf16[256,2048]{1,0:T(8,128)(2,1)} %get-tuple-element.171), channel_id=1, source_target_pairs={{0,1},{1,0},{2,3},{3,2},{4,5},{5,4},{6,7},{7,6},{8,9},{9,8},{10,11... | collective-permute-start | bytes 3145736 | tf_op jit(solution)/shard_map/ppermute | solution.py:237
  176.3 58.2 %collective-permute-start.1 = (bf16[256,2048]{1,0:T(8,128)(2,1)S(1)}, bf16[256,2048]{1,0:T(8,128)(2,1)}, u32[]{:S(2)}, u32[]{:S(2)}) collective-permute-start(bf16[256,2048]{1,0:T(8,128)(2,1)S(1)} %get-tuple-element.170), channel_id=1, source_target_pairs={{0,1},{1,0},{2,3},{3,2},{4,5},{5,4},{6,7},{7,6},{8,9},{9,8},{10,11... | collective-permute-start | bytes 3145736 | tf_op jit(solution)/shard_map/ppermute | solution.py:237
  178.4 54.9 %collective-permute-start.6 = (bf16[256,1024]{1,0:T(8,128)(2,1)}, bf16[256,1024]{1,0:T(8,128)(2,1)S(1)}, u32[]{:S(2)}, u32[]{:S(2)}) collective-permute-start(bf16[256,1024]{1,0:T(8,128)(2,1)} %param.31), channel_id=1, source_target_pairs={{0,2},{1,3},{2,0},{3,1},{4,6},{5,7},{6,4},{7,5},{8,10},{9,11},{10,... | collective-permute-start | bytes 1572872 | tf_op jit(solution)/shard_map/ppermute | solution.py:243
  254.2 224.6 %all-gather.14.cloned.1.call-start = ((), (), s32[]{:S(2)}) async-start(), calls=%async_computation.11 | async-start | bytes 9437184 | tf_op jit(solution)/shard_map/all_gather | solution.py:311
  254.3 25.6 %collective-permute-start.7 = (bf16[256,1024]{0,1:T(8,128)(2,1)}, bf16[256,1024]{0,1:T(8,128)(2,1)S(1)}, u32[]{:S(2)}, u32[]{:S(2)}) collective-permute-start(bf16[256,1024]{0,1:T(8,128)(2,1)} %bitcast.105), channel_id=1, source_target_pairs={{0,2},{1,3},{2,0},{3,1},{4,6},{5,7},{6,4},{7,5},{8,10},{9,11},{10,... | collective-permute-start | bytes 1572872 | tf_op jit(solution)/shard_map/ppermute | solution.py:243
  281.9 19.1 %copy-start.38 = (s32[2,1,1024]{2,1,0:T(1,128)S(1)}, s32[2,1,1024]{2,1,0:T(1,128)}, u32[]{:S(2)}) copy-start(s32[2,1,1024]{2,1,0:T(1,128)} %param.19) | copy-start | bytes 24580
  300.7 401.1 %reduce-scatter.8.cloned.1.call-start = ((), (), s32[]{:S(2)}) async-start(), calls=%async_computation.13 | async-start | bytes 9437184 | tf_op jit(solution)/shard_map/reduce_scatter | solution.py:397
  346.4 69.4 %collective-permute-start.5 = (bf16[512,2048]{1,0:T(8,128)(2,1)}, bf16[512,2048]{1,0:T(8,128)(2,1)}, u32[]{:S(2)}, u32[]{:S(2)}) collective-permute-start(bf16[512,2048]{1,0:T(8,128)(2,1)} %convolution_convert_fusion.7), channel_id=1, source_target_pairs={{0,1},{1,0},{2,3},{3,2},{4,5},{5,4},{6,7},{7,6},{8,9},{9,8},{10,11... | collective-permute-start | bytes 6291464 | tf_op jit(solution)/shard_map/ppermute | solution.py:237
  347.6 259.2 %copy-start.10 = (bf16[256,2048]{1,0:T(8,128)(2,1)}, bf16[256,2048]{1,0:T(8,128)(2,1)S(1)}, u32[]{:S(2)}) copy-start(bf16[256,2048]{1,0:T(8,128)(2,1)S(1)} %get-tuple-element.154) | copy-start | bytes 3145732
  348.1 67.8 %copy-start.33 = (f32[512]{0:T(512)}, f32[512]{0:T(512)S(1)}, u32[]{:S(2)}) copy-start(f32[512]{0:T(512)S(1)} %broadcast_multiply_fusion.1) | copy-start | bytes 6148
  348.1 75.7 %collective-permute-start.9 = (bf16[256,2048]{1,0:T(8,128)(2,1)}, bf16[256,2048]{1,0:T(8,128)(2,1)}, u32[]{:S(2)}, u32[]{:S(2)}) collective-permute-start(bf16[256,2048]{1,0:T(8,128)(2,1)} %get-tuple-element.65), channel_id=1, source_target_pairs={{0,2},{1,3},{2,0},{3,1},{4,6},{5,7},{6,4},{7,5},{8,10},{9,11},{10,... | collective-permute-start | bytes 3145736 | tf_op jit(solution)/shard_map/ppermute | solution.py:243
  421.7 48.6 %collective-permute-start.8 = (bf16[512,2048]{1,0:T(8,128)(2,1)S(1)}, bf16[512,2048]{1,0:T(8,128)(2,1)}, u32[]{:S(2)}, u32[]{:S(2)}) collective-permute-start(bf16[512,2048]{1,0:T(8,128)(2,1)S(1)} %add_convert_fusion.1), channel_id=1, source_target_pairs={{0,1},{1,0},{2,3},{3,2},{4,5},{5,4},{6,7},{7,6},{8,9},{9,8},{10,11... | collective-permute-start | bytes 6291464 | tf_op jit(solution)/shard_map/ppermute | solution.py:237
  421.7 71.1 %collective-permute-start.10 = (bf16[256,2048]{1,0:T(8,128)(2,1)S(1)}, bf16[256,2048]{1,0:T(8,128)(2,1)}, u32[]{:S(2)}, u32[]{:S(2)}) collective-permute-start(bf16[256,2048]{1,0:T(8,128)(2,1)S(1)} %get-tuple-element.154), channel_id=1, source_target_pairs={{0,1},{1,0},{2,3},{3,2},{4,5},{5,4},{6,7},{7,6},{8,9},{9,8},{10,11... | collective-permute-start | bytes 3145736 | tf_op jit(solution)/shard_map/ppermute | solution.py:237
  423.7 88.8 %collective-permute-start.11 = (bf16[256,2048]{1,0:T(8,128)(2,1)}, bf16[256,2048]{1,0:T(8,128)(2,1)}, u32[]{:S(2)}, u32[]{:S(2)}) collective-permute-start(bf16[256,2048]{1,0:T(8,128)(2,1)} %collective-permute-done.9), channel_id=1, source_target_pairs={{0,1},{1,0},{2,3},{3,2},{4,5},{5,4},{6,7},{7,6},{8,9},{9,8},{10,11... | collective-permute-start | bytes 3145736 | tf_op jit(solution)/shard_map/ppermute | solution.py:237
  423.8 46.5 %copy-start.52 = (bf16[2048,2048]{1,0:T(8,128)(2,1)S(1)}, bf16[2048,2048]{1,0:T(8,128)(2,1)}, u32[]{:S(2)}) copy-start(bf16[2048,2048]{1,0:T(8,128)(2,1)} %all-gather.12.cloned.1.call-done) | copy-start | bytes 25165828
  478.8 33.7 %copy-start.51 = (bf16[2048,2048]{0,1:T(8,128)(2,1)S(1)}, bf16[2048,2048]{0,1:T(8,128)(2,1)}, u32[]{:S(2)}) copy-start(bf16[2048,2048]{0,1:T(8,128)(2,1)} %all-gather.14.cloned.1.call-done) | copy-start | bytes 25165828
  478.8 33.7 %copy-start.54 = (f32[512,2048]{1,0:T(8,128)S(1)}, f32[512,2048]{1,0:T(8,128)}, u32[]{:S(2)}) copy-start(f32[512,2048]{1,0:T(8,128)} %get-tuple-element.191) | copy-start | bytes 12582916
  487.8 70.1 %copy-start.20 = (bf16[512,2048]{1,0:T(8,128)(2,1)}, bf16[512,2048]{1,0:T(8,128)(2,1)S(1)}, u32[]{:S(2)}) copy-start(bf16[512,2048]{1,0:T(8,128)(2,1)S(1)} %multiply_convert_fusion.1) | copy-start | bytes 6291460
  534.3 228.0 %reduce-scatter.6.cloned.1.call-start = ((), (), s32[]{:S(2)}) async-start(), calls=%async_computation.12 | async-start | bytes 9437184 | tf_op jit(solution)/shard_map/reduce_scatter | solution.py:397
  549.2 262.5 %reduce-scatter.10.cloned.1.call-start = ((), (), s32[]{:S(2)}) async-start(), calls=%async_computation.14 | async-start | bytes 14155776 | tf_op jit(solution)/shard_map/reduce_scatter | solution.py:397
  557.8 45.0 %collective-permute-start.12 = (bf16[512,2048]{1,0:T(8,128)(2,1)S(1)}, bf16[512,2048]{1,0:T(8,128)(2,1)S(1)}, u32[]{:S(2)}, u32[]{:S(2)}) collective-permute-start(bf16[512,2048]{1,0:T(8,128)(2,1)S(1)} %convolution_convert_fusion.5), channel_id=1, source_target_pairs={{0,1},{1,0},{2,3},{3,2},{4,5},{5,4},{6,7},{7,6},{8,9},{9,8},{10,11... | collective-permute-start | bytes 6291464 | tf_op jit(solution)/shard_map/ppermute | solution.py:237
  557.9 44.9 %copy-start.1 = (f32[512,2048]{1,0:T(8,128)S(1)}, f32[512,2048]{1,0:T(8,128)}, u32[]{:S(2)}) copy-start(f32[512,2048]{1,0:T(8,128)} %copy-done) | copy-start | bytes 12582916
  609.6 44.5 %collective-permute-start.13 = (bf16[512,2048]{1,0:T(8,128)(2,1)S(1)}, bf16[512,2048]{1,0:T(8,128)(2,1)S(1)}, u32[]{:S(2)}, u32[]{:S(2)}) collective-permute-start(bf16[512,2048]{1,0:T(8,128)(2,1)S(1)} %fusion.47), channel_id=1, source_target_pairs={{0,1},{1,0},{2,3},{3,2},{4,5},{5,4},{6,7},{7,6},{8,9},{9,8},{10,11... | collective-permute-start | bytes 6291464 | tf_op jit(solution)/shard_map/ppermute | solution.py:237
  660.2 22.2 %copy-start.15 = (bf16[256,2048]{1,0:T(8,128)(2,1)S(1)}, bf16[256,2048]{1,0:T(8,128)(2,1)}, u32[]{:S(2)}) copy-start(bf16[256,2048]{1,0:T(8,128)(2,1)} %copy-done.14) | copy-start | bytes 3145732
  701.8 195.3 %reduce-scatter.14.cloned.1.call-start = ((), (), s32[]{:S(2)}) async-start(), calls=%async_computation.16 | async-start | bytes 9437184 | tf_op jit(solution)/shard_map/reduce_scatter | solution.py:397
  717.7 316.7 %reduce-scatter.12.cloned.1.call-start = ((), (), s32[]{:S(2)}) async-start(), calls=%async_computation.15 | async-start | bytes 14155776 | tf_op jit(solution)/shard_map/reduce_scatter | solution.py:397
  717.8 44.5 %collective-permute-start.14 = (bf16[512,2048]{1,0:T(8,128)(2,1)}, bf16[512,2048]{1,0:T(8,128)(2,1)S(1)}, u32[]{:S(2)}, u32[]{:S(2)}) collective-permute-start(bf16[512,2048]{1,0:T(8,128)(2,1)} %convolution_convert_fusion.6), channel_id=1, source_target_pairs={{0,1},{1,0},{2,3},{3,2},{4,5},{5,4},{6,7},{7,6},{8,9},{9,8},{10,11... | collective-permute-start | bytes 6291464 | tf_op jit(solution)/shard_map/ppermute | solution.py:237
  763.8 20.8 %copy-start.27 = (bf16[256,2048]{1,0:T(8,128)(2,1)S(1)}, bf16[256,2048]{1,0:T(8,128)(2,1)}, u32[]{:S(2)}) copy-start(bf16[256,2048]{1,0:T(8,128)(2,1)} %reduce-scatter.6.cloned.1.call-done) | copy-start | bytes 3145732
  763.8 20.9 %copy-start.26 = (bf16[256,2048]{1,0:T(8,128)(2,1)S(1)}, bf16[256,2048]{1,0:T(8,128)(2,1)}, u32[]{:S(2)}) copy-start(bf16[256,2048]{1,0:T(8,128)(2,1)} %reduce-scatter.8.cloned.1.call-done) | copy-start | bytes 3145732
  763.8 20.7 %collective-permute-start.16 = (bf16[256,1024]{1,0:T(8,128)(2,1)S(1)}, bf16[256,1024]{1,0:T(8,128)(2,1)S(1)}, u32[]{:S(2)}, u32[]{:S(2)}) collective-permute-start(bf16[256,1024]{1,0:T(8,128)(2,1)S(1)} %slice.182), channel_id=1, source_target_pairs={{0,2},{1,3},{2,0},{3,1},{4,6},{5,7},{6,4},{7,5},{8,10},{9,11},{10,... | collective-permute-start | bytes 1572872 | tf_op jit(solution)/shard_map/ppermute | solution.py:243
  769.4 65.9 %copy-start.12 = (bf16[512,2048]{1,0:T(8,128)(2,1)}, bf16[512,2048]{1,0:T(8,128)(2,1)S(1)}, u32[]{:S(2)}) copy-start(bf16[512,2048]{1,0:T(8,128)(2,1)S(1)} %add_add_fusion.3) | copy-start | bytes 6291460
  785.6 23.5 %collective-permute-start.18 = (bf16[256,1024]{1,0:T(8,128)(2,1)}, bf16[256,1024]{1,0:T(8,128)(2,1)}, u32[]{:S(2)}, u32[]{:S(2)}) collective-permute-start(bf16[256,1024]{1,0:T(8,128)(2,1)} %slice.184), channel_id=1, source_target_pairs={{0,2},{1,3},{2,0},{3,1},{4,6},{5,7},{6,4},{7,5},{8,10},{9,11},{10,... | collective-permute-start | bytes 1572872 | tf_op jit(solution)/shard_map/ppermute | solution.py:243
  836.4 141.4 %collective-permute-start.15 = (bf16[256,2048]{1,0:T(8,128)(2,1)}, bf16[256,2048]{1,0:T(8,128)(2,1)}, u32[]{:S(2)}, u32[]{:S(2)}) collective-permute-start(bf16[256,2048]{1,0:T(8,128)(2,1)} %slice.179), channel_id=1, source_target_pairs={{0,2},{1,3},{2,0},{3,1},{4,6},{5,7},{6,4},{7,5},{8,10},{9,11},{10,... | collective-permute-start | bytes 3145736 | tf_op jit(solution)/shard_map/ppermute | solution.py:243
  864.6 93.3 %collective-permute-start.17 = (bf16[512,2048]{1,0:T(8,128)(2,1)}, bf16[512,2048]{1,0:T(8,128)(2,1)}, u32[]{:S(2)}, u32[]{:S(2)}) collective-permute-start(bf16[512,2048]{1,0:T(8,128)(2,1)} %add_convert_fusion), channel_id=1, source_target_pairs={{0,1},{1,0},{2,3},{3,2},{4,5},{5,4},{6,7},{7,6},{8,9},{9,8},{10,11... | collective-permute-start | bytes 6291464 | tf_op jit(solution)/shard_map/ppermute | solution.py:237
  878.2 86.1 %copy-start.3 = (bf16[256,2048]{1,0:T(8,128)(2,1)S(1)}, bf16[256,2048]{1,0:T(8,128)(2,1)}, u32[]{:S(2)}) copy-start(bf16[256,2048]{1,0:T(8,128)(2,1)} %copy-done.2) | copy-start | bytes 3145732
  878.2 86.1 %copy-start.5 = (bf16[256,2048]{1,0:T(8,128)(2,1)S(1)}, bf16[256,2048]{1,0:T(8,128)(2,1)}, u32[]{:S(2)}) copy-start(bf16[256,2048]{1,0:T(8,128)(2,1)} %copy-done.4) | copy-start | bytes 3145732
  878.2 86.1 %copy-start.31 = (f32[2048]{0:T(1024)S(1)}, f32[2048]{0:T(1024)}, u32[]{:S(2)}) copy-start(f32[2048]{0:T(1024)} %copy-done.30) | copy-start | bytes 24580
  878.2 86.1 %copy-start.34 = (f32[512]{0:T(512)S(1)}, f32[512]{0:T(512)}, u32[]{:S(2)}) copy-start(f32[512]{0:T(512)} %copy-done.33) | copy-start | bytes 6148
  878.2 86.0 %collective-permute-start.19 = (bf16[256,3072]{1,0:T(8,128)(2,1)}, bf16[256,3072]{1,0:T(8,128)(2,1)}, u32[]{:S(2)}, u32[]{:S(2)}) collective-permute-start(bf16[256,3072]{1,0:T(8,128)(2,1)} %reduce-scatter.10.cloned.1.call-done), channel_id=1, source_target_pairs={{0,2},{1,3},{2,0},{3,1},{4,6},{5,7},{6,4},{7,5},{8,10},{9,11},{10,... | collective-permute-start | bytes 4718600 | tf_op jit(solution)/shard_map/ppermute | solution.py:243
  899.0 69.6 %copy-start.8 = (f32[512,2048]{1,0:T(8,128)S(1)}, f32[512,2048]{1,0:T(8,128)}, u32[]{:S(2)}) copy-start(f32[512,2048]{1,0:T(8,128)} %fusion.42) | copy-start | bytes 12582916
  899.0 90.0 %collective-permute-start.21 = (bf16[256,1024]{1,0:T(8,128)(2,1)}, bf16[256,1024]{1,0:T(8,128)(2,1)}, u32[]{:S(2)}, u32[]{:S(2)}) collective-permute-start(bf16[256,1024]{1,0:T(8,128)(2,1)} %slice.194), channel_id=1, source_target_pairs={{0,2},{1,3},{2,0},{3,1},{4,6},{5,7},{6,4},{7,5},{8,10},{9,11},{10,... | collective-permute-start | bytes 1572872 | tf_op jit(solution)/shard_map/ppermute | solution.py:243
  977.7 52.0 %collective-permute-start.20 = (bf16[256,2048]{1,0:T(8,128)(2,1)S(1)}, bf16[256,2048]{1,0:T(8,128)(2,1)}, u32[]{:S(2)}, u32[]{:S(2)}) collective-permute-start(bf16[256,2048]{1,0:T(8,128)(2,1)S(1)} %slice.225), channel_id=1, source_target_pairs={{0,2},{1,3},{2,0},{3,1},{4,6},{5,7},{6,4},{7,5},{8,10},{9,11},{10,... | collective-permute-start | bytes 3145736 | tf_op jit(solution)/shard_map/ppermute | solution.py:243
  984.2 44.3 %all-to-all-start.1 = ((f32[32,6,128]{2,1,0:T(8,128)}), f32[32,6,128]{2,1,0:T(8,128)S(1)}, u32[]{:S(2)}, u32[]{:S(2)}) async-start(f32[32,6,128]{2,1,0:T(8,128)} %reshape.219), calls=%async_computation.4 | async-start | bytes 262144 | tf_op jit(solution)/shard_map/all_to_all | solution.py:284
  (31 other events, 140.3 us)
Sparse Core Ops, SparseCore 0:
  12.7 74.7 all-gather.7
  135.4 71.2 all-gather.5
  209.1 55.2 all-gather.9
  266.2 54.2 all-gather.11
  322.2 55.8 all-gather.13
  534.4 68.1 reduce-scatter.7
  606.1 71.4 reduce-scatter.5
  701.9 90.8 reduce-scatter.9
  796.3 71.4 reduce-scatter.13
  871.2 92.2 reduce-scatter.11
